TPU v7x, 128 devices: a whole 4x4x4 slice. The times are simulated.
128 devices in a mesh: cfg: 2 (over x_lo), seq: 32 (over y, z, core), req: 2 (over x_hi).
Axes of the slice: x: 4 (x_hi: 2, x_lo: 2; x = x_hi * 2 + x_lo), y: 4, z: 4, core: 2. Of those that a mesh axis runs over, the one named last changes fastest.
Arguments:
- latents: float32 [4096, 8, 64], P('seq', 'req', 'cfg'), may hold values from -6 to 6
- hidden_img: bfloat16 [2, 4096, 8, 3072], P('cfg', 'seq', 'req'), may hold values from -3 to 3
- query_img: bfloat16 [2, 4096, 8, 2048], P('cfg', 'seq', 'req'), may hold values from -12 to 12
- key_img: bfloat16 [2, 4096, 8, 2048], P('cfg', 'seq', 'req'), may hold values from -12 to 12
- value_img: bfloat16 [2, 4096, 8, 2048], P('cfg', 'seq', 'req'), may hold values from -6 to 6
- key_txt: bfloat16 [2, 512, 8, 2048], P('cfg', 'seq', 'req'), may hold values from -12 to 12
- value_txt: bfloat16 [2, 512, 8, 2048], P('cfg', 'seq', 'req'), may hold values from -6 to 6
- text_len: int32 [2, 8], P('cfg', 'req'), may hold values from 1 to 512, 2048 in all within a row
- img_ids: int32 [3, 4096], P(None, 'seq'), may hold values from 0 to 63
- t_index: int32 [8], P('req'), may hold values from 1 to 28
- g_index: int32 [8], P('req'), may hold values from 0 to 8
- proj_weight: bfloat16 [2048, 3072], P(('cfg', 'seq')), may hold values from -0.125 to 0.125
- attn_gate: float32 [2, 8, 3072], P('cfg', 'req'), may hold values from -4 to 4
- final_shift: float32 [2, 8, 3072], P('cfg', 'req'), may hold values from -3 to 3
- final_scale: float32 [2, 8, 3072], P('cfg', 'req'), may hold values from -2 to 2
- out_weight: bfloat16 [3072, 64], replicated, may hold values from -0.109375 to 0.109375
- out_bias: float32 [64], replicated, may hold values from -3 to 3
Outputs:
- next_latents: float32 [4096, 8, 64], P('seq', 'req', 'cfg')
- denoised: float32 [4096, 8, 64], P('seq', 'req', 'cfg')
Inputs may be any that keep to these rules, and one draw needn't show every extreme that they name: `text_len`: in each half the lengths of all 8 prompts sum to 2048 and the largest is 512.
All inputs are finite; a program needn't handle non-finite values. No bound on the sum of `text_len` on one device may be relied on, other than what follows from the above.
Results may differ from a plain program's by a relative error of at most 0.0066.
Values may be sent and summed in bfloat16 or wider, within the bound.
A program may use at most 128 MiB of HBM per device.

v0:
```python
import math

import jax
import jax.numpy as jnp
from jax import lax
from jax.sharding import PartitionSpec as P

HSIZE = 128
STEPS = 28


def partner_2(value, axis, distance):
    mask = 2**distance
    pairs = [(source, source ^ mask) for source in range(lax.axis_size(axis))]
    return lax.ppermute(value, axis, pairs)


def rope_angles(position_ids):
    pieces = []
    for axis_number, extent in enumerate((HSIZE // 8, 7 * HSIZE // 16, 7 * HSIZE // 16)):
        freq = jnp.power(
            jnp.float32(10000.0), -2.0 * jnp.arange(extent // 2, dtype=jnp.float32) / extent
        )
        pieces.append(position_ids[axis_number].astype(jnp.float32)[:, None] * freq[None, :])
    return jnp.concatenate(pieces, axis=1)


def rotate(values, angle):
    half_width = values.shape[-1] // 2
    first = values[..., :half_width]
    second = values[..., half_width:]
    cosine = jnp.cos(angle)
    sine = jnp.sin(angle)
    return jnp.concatenate(
        [first * cosine - second * sine, first * sine + second * cosine], axis=-1
    )


def attend(queries, keys_img, values_img, keys_txt, values_txt, length):
    factor = HSIZE ** (-0.5)
    score_img = jnp.dot(queries, keys_img.T, preferred_element_type=jnp.float32) * factor
    score_txt = jnp.dot(queries, keys_txt.T, preferred_element_type=jnp.float32) * factor
    live = jnp.arange(keys_txt.shape[0], dtype=jnp.int32) < length
    score_txt = jnp.where(live[None, :], score_txt, jnp.float32(-1e30))
    top = jnp.maximum(jnp.max(score_img, axis=1), jnp.max(score_txt, axis=1))
    exp_img = jnp.exp(score_img - top[:, None])
    exp_txt = jnp.where(live[None, :], jnp.exp(score_txt - top[:, None]), jnp.float32(0.0))
    total = jnp.sum(exp_img, axis=1) + jnp.sum(exp_txt, axis=1)
    summed = jnp.dot(exp_img.astype(jnp.bfloat16), values_img, preferred_element_type=jnp.float32)
    summed = summed + jnp.dot(
        exp_txt.astype(jnp.bfloat16), values_txt, preferred_element_type=jnp.float32
    )
    return (summed / total[:, None]).astype(jnp.bfloat16)


def attend_blocks(queries, keys_img, values_img, keys_txt, values_txt, length):
    query_rows = queries.shape[0]
    block_rows = math.gcd(query_rows, 512)
    blocked = queries.reshape(query_rows // block_rows, block_rows, queries.shape[1])

    def one_block(block):
        return attend(block, keys_img, values_img, keys_txt, values_txt, length)

    return lax.map(one_block, blocked).reshape(query_rows, queries.shape[1])


def roster(fraction):
    return 3.0 * fraction / (1.0 + 2.0 * fraction)


def shards(
    latents,
    hidden_img,
    query_img,
    key_img,
    value_img,
    key_txt,
    value_txt,
    text_len,
    img_ids,
    t_index,
    g_index,
    proj_weight,
    attn_gate,
    final_shift,
    final_scale,
    out_weight,
    out_bias,
):
    img_rows = query_img.shape[1]
    prompt_count = query_img.shape[2]
    feature_width = query_img.shape[3]
    head_count = feature_width // HSIZE
    text_rows = key_txt.shape[1]
    members = prompt_count * head_count
    angle = rope_angles(img_ids)[:, None, :]
    rot_query = rotate(
        query_img[0].reshape(img_rows, members, HSIZE).astype(jnp.float32), angle
    ).astype(jnp.bfloat16)
    rot_key = rotate(
        key_img[0].reshape(img_rows, members, HSIZE).astype(jnp.float32), angle
    ).astype(jnp.bfloat16)
    vals = value_img[0].reshape(img_rows, members, HSIZE)
    text_keys = key_txt[0].reshape(text_rows, members, HSIZE)
    text_vals = value_txt[0].reshape(text_rows, members, HSIZE)
    all_query, all_key, all_vals, all_text_keys, all_text_vals = (
        lax.all_to_all(rot_query, "seq", split_axis=1, concat_axis=0, tiled=True),
        lax.all_to_all(rot_key, "seq", split_axis=1, concat_axis=0, tiled=True),
        lax.all_to_all(vals, "seq", split_axis=1, concat_axis=0, tiled=True),
        lax.all_to_all(text_keys, "seq", split_axis=1, concat_axis=0, tiled=True),
        lax.all_to_all(text_vals, "seq", split_axis=1, concat_axis=0, tiled=True),
    )
    held = all_query.shape[1]
    first_member = lax.axis_index("seq") * held
    lengths = text_len[0]
    prompt_slots = jnp.arange(prompt_count, dtype=jnp.int32)
    results = []
    for member in range(held):
        prompt_of = (first_member + member) // head_count
        length = jnp.sum(jnp.where(prompt_slots == prompt_of, lengths, 0))
        results.append(
            attend_blocks(
                all_query[:, member],
                all_key[:, member],
                all_vals[:, member],
                all_text_keys[:, member],
                all_text_vals[:, member],
                length,
            )
        )
    attended = jnp.stack(results, axis=1)
    returned = lax.all_to_all(attended, "seq", split_axis=0, concat_axis=1, tiled=True)
    flat_attended = returned.reshape(img_rows * prompt_count, feature_width)
    projected = jnp.dot(
        flat_attended,
        lax.all_gather(proj_weight, ("cfg", "seq"), axis=0, tiled=True),
        preferred_element_type=jnp.float32,
    )
    projected = projected.reshape(img_rows, prompt_count, hidden_img.shape[3])
    residual = hidden_img[0].astype(jnp.float32) + attn_gate[0][None] * projected
    mean_value = jnp.mean(residual, axis=-1, keepdims=True)
    centred = residual - mean_value
    spread = jnp.mean(centred * centred, axis=-1, keepdims=True)
    normed = centred * lax.rsqrt(spread + 1e-06)
    modulated = (normed * (1.0 + final_scale[0][None]) + final_shift[0][None]).astype(jnp.bfloat16)
    velocity = (
        jnp.dot(
            modulated.reshape(img_rows * prompt_count, hidden_img.shape[3]),
            out_weight,
            preferred_element_type=jnp.float32,
        )
        + out_bias[None, :]
    )
    velocity = velocity.reshape(img_rows, prompt_count, out_weight.shape[1])
    kept = latents.shape[2]
    strength = (1.0 + 0.5 * g_index.astype(jnp.float32))[None, :, None]
    partner = partner_2(velocity, "cfg", 0)
    own_half = lax.axis_index("cfg")
    cond_full = jnp.where(own_half == 0, velocity, partner)
    uncond_full = jnp.where(own_half == 0, partner, velocity)
    guided_full = uncond_full + strength * (cond_full - uncond_full)
    guided = lax.dynamic_slice_in_dim(guided_full, own_half * kept, kept, 2)
    moment = t_index.astype(jnp.float32)
    sigma_now = roster(moment / STEPS)[None, :, None]
    sigma_next = roster((moment - 1.0) / STEPS)[None, :, None]
    next_latents = latents + (sigma_next - sigma_now) * guided
    denoised = latents - sigma_now * guided
    return (next_latents, denoised)


def solution(mesh):
    placed = (
        P("seq", "req", "cfg"),
        P("cfg", "seq", "req", None),
        P("cfg", "seq", "req", None),
        P("cfg", "seq", "req", None),
        P("cfg", "seq", "req", None),
        P("cfg", "seq", "req", None),
        P("cfg", "seq", "req", None),
        P("cfg", "req"),
        P(None, "seq"),
        P("req"),
        P("req"),
        P(("cfg", "seq"), None),
        P("cfg", "req", None),
        P("cfg", "req", None),
        P("cfg", "req", None),
        P(),
        P(),
    )
    return jax.shard_map(
        shards,
        mesh=mesh,
        in_specs=placed,
        out_specs=(P("seq", "req", "cfg"), P("seq", "req", "cfg")),
        check_vma=False,
    )
```

profile of v0, /device:TPU:6, one launch (start us, length us, event | category | flops | bytes accessed | tf_op | source)
XLA Modules:
  0.0 399.4 jit_solution(1739430919779507370)
XLA Ops:
  9.2 8.3 %all-to-all-start.2 = ((bf16[16,64,128]{2,0,1:T(8,128)(2,1)}), bf16[16,64,128]{2,0,1:T(8,128)(2,1)S(1)}, u32[]{:S(2)}, u32[]{:S(2)}) async-start(bf16[16,64,128]{2,0,1:T(8,128)(2,1)} %copy.81), calls=%async_computation.2 | async-start | bytes 524288 | tf_op jit(solution)/shard_map/all_to_all | solution.py:110
  18.4 3.4 copy.76
  24.3 3.4 copy.78
  31.6 7.4 %all-to-all-start.4 = ((bf16[16,64,128]{2,0,1:T(8,128)(2,1)}), bf16[16,64,128]{2,0,1:T(8,128)(2,1)S(1)}, u32[]{:S(2)}, u32[]{:S(2)}) async-start(bf16[16,64,128]{2,0,1:T(8,128)(2,1)} %copy.86), calls=%async_computation.4 | async-start | bytes 524288 | tf_op jit(solution)/shard_map/all_to_all | solution.py:111
  39.1 5.8 %subtract_convert_fusion = (bf16[128,64,64]{0,2,1:T(8,128)(2,1)S(1)}, bf16[128,64,64]{0,2,1:T(8,128)(2,1)S(1)}, bf16[128,64,64]{0,2,1:T(8,128)(2,1)S(1)}, bf16[128,64,64]{0,2,1:T(8,128)(2,1)}) fusion(f32[128,64,128]{0,2,1:T(8,128)} %convert.20, f32[128,64]{0,1:T(8,128)S(1)} %get-tuple-element.159, f32[128,64]{0,1:T(8,128)S(1)} %get-tuple-element.158, ...), kind=kLoop, calls=%fused_computation.65 | loop fusion | flops 8388608 | bytes 12648448 | tf_op jit(solution)/shard_map/convert.3
  48.7 5.8 %all-to-all-start.1 = ((bf16[128,64,128]{0,2,1:T(8,128)(2,1)}), bf16[128,64,128]{0,2,1:T(8,128)(2,1)S(1)}, u32[]{:S(2)}, u32[]{:S(2)}) async-start(bf16[128,64,128]{0,2,1:T(8,128)(2,1)} %pad_maximum_fusion.1), calls=%async_computation.1 | async-start | bytes 4194304 | tf_op jit(solution)/shard_map/all_to_all | solution.py:108
  54.4 4.5 %copy.83 = bf16[1,128,4,2048]{1,3,2,0:T(8,128)(2,1)} copy(bf16[1,128,4,2048]{3,2,1,0:T(4,128)(2,1)} %param.25) | data formatting | bytes 4194304 | tf_op args[4]
  59.0 24.4 %all-to-all-done.1 = bf16[128,64,128]{0,2,1:T(8,128)(2,1)S(1)} async-done(((bf16[128,64,128]{0,2,1:T(8,128)(2,1)}), bf16[128,64,128]{0,2,1:T(8,128)(2,1)S(1)}, u32[]{:S(2)}, u32[]{:S(2)}) %all-to-all-start.1) | async-done | bytes 2097184 | tf_op jit(solution)/shard_map/all_to_all | solution.py:108
  83.4 4.8 %all-to-all-start.3 = ((bf16[128,64,128]{0,2,1:T(8,128)(2,1)}), bf16[128,64,128]{0,2,1:T(8,128)(2,1)}, u32[]{:S(2)}, u32[]{:S(2)}) async-start(bf16[128,64,128]{0,2,1:T(8,128)(2,1)} %bitcast.141), calls=%async_computation.3 | async-start | bytes 4194304 | tf_op jit(solution)/shard_map/all_to_all | solution.py:109
  88.2 2.7 pad_maximum_fusion
  90.9 26.1 %all-to-all-done.3 = bf16[128,64,128]{0,2,1:T(8,128)(2,1)} async-done(((bf16[128,64,128]{0,2,1:T(8,128)(2,1)}), bf16[128,64,128]{0,2,1:T(8,128)(2,1)}, u32[]{:S(2)}, u32[]{:S(2)}) %all-to-all-start.3) | async-done | bytes 2097184 | tf_op jit(solution)/shard_map/all_to_all | solution.py:109
  117.0 4.8 %all-to-all-start = ((bf16[128,64,128]{0,2,1:T(8,128)(2,1)}), bf16[128,64,128]{0,2,1:T(8,128)(2,1)}, u32[]{:S(2)}, u32[]{:S(2)}) async-start(bf16[128,64,128]{0,2,1:T(8,128)(2,1)} %pad_maximum_fusion), calls=%async_computation | async-start | bytes 4194304 | tf_op jit(solution)/shard_map/all_to_all | solution.py:107
  124.1 2.9 copy.80
  127.0 4.1 %copy.85 = bf16[32,128,2,128]{3,1,0,2:T(8,128)(2,1)} copy(bf16[32,128,2,128]{1,3,2,0:T(8,128)(2,1)} %bitcast.30) | data formatting | bytes 4194304 | tf_op jit(solution)/shard_map/all_to_all | solution.py:109
  131.1 24.4 %all-to-all-done = bf16[128,64,128]{0,2,1:T(8,128)(2,1)} async-done(((bf16[128,64,128]{0,2,1:T(8,128)(2,1)}), bf16[128,64,128]{0,2,1:T(8,128)(2,1)}, u32[]{:S(2)}, u32[]{:S(2)}) %all-to-all-start) | async-done | bytes 2097184 | tf_op jit(solution)/shard_map/all_to_all | solution.py:107
  155.5 3.1 copy.77
  164.1 72.1 %while.20 = (s32[]{:T(128)}, bf16[8,512,128]{2,1,0:T(8,128)(2,1)}, bf16[8,512,128]{2,1,0:T(8,128)(2,1)}, bf16[4096,128]{1,0:T(8,128)(2,1)}, s32[]{:T(128)}, /*in...) while((s32[]{:T(128)}, bf16[8,512,128]{2,1,0:T(8,128)(2,1)}, ...), condition=%wide.region_6.7_spmd, body=%wide.region_1.6_spmd.sunk | while | flops 1227292160 | bytes 32147068 | solution.py:64
  166.0 2.6 multiply_reduce_fusion.5
  184.0 2.7 multiply_reduce_fusion.5
  193.0 2.7 multiply_reduce_fusion.5
  202.0 2.7 multiply_reduce_fusion.5
  211.1 2.7 multiply_reduce_fusion.5
  220.1 2.7 multiply_reduce_fusion.5
  229.1 2.6 multiply_reduce_fusion.5
  236.3 64.1 %while.21 = (s32[]{:T(128)}, bf16[8,512,128]{2,1,0:T(8,128)(2,1)S(1)}, bf16[8,512,128]{2,1,0:T(8,128)(2,1)}, bf16[4096,128]{1,0:T(8,128)(2,1)S(1)}, s32[]{:T(128...) while((s32[]{:T(128)}, ...), condition=%wide.region_13.14_spmd, body=%wide.region_8.13_spmd.sunk | while | flops 1227292160 | bytes 32146560 | solution.py:64
  301.9 18.1 %copy.88 = bf16[4096,2,128]{2,1,0:T(2,128)(2,1)} copy(bf16[4096,2,128]{2,0,1:T(8,128)(2,1)S(1)} %pad_maximum_fusion.2) | data formatting | bytes 4194304 | tf_op jit(solution)/shard_map/stack | solution.py:131
  320.0 7.0 %all-to-all-start.5 = ((bf16[4096,2,128]{2,1,0:T(2,128)(2,1)}), bf16[4096,2,128]{2,1,0:T(2,128)(2,1)S(1)}, u32[]{:S(2)}, u32[]{:S(2)}) async-start(bf16[4096,2,128]{2,1,0:T(2,128)(2,1)} %copy.88), calls=%async_computation.5 | async-start | bytes 4194304 | tf_op jit(solution)/shard_map/all_to_all | solution.py:132
  327.9 27.8 %all-to-all-done.5 = bf16[4096,2,128]{2,1,0:T(2,128)(2,1)S(1)} async-done(((bf16[4096,2,128]{2,1,0:T(2,128)(2,1)}), bf16[4096,2,128]{2,1,0:T(2,128)(2,1)S(1)}, u32[]{:S(2)}, u32[]{:S(2)}) %all-to-all-start.5) | async-done | bytes 2097184 | tf_op jit(solution)/shard_map/all_to_all | solution.py:132
  357.3 3.2 copy.90
  360.6 11.7 %fusion.59 = (f32[128,4]{0,1:T(4,128)S(1)}, f32[128,4,3072]{2,0,1:T(8,128)S(1)}) fusion(bf16[128,4,2048]{0,2,1:T(8,128)(2,1)S(1)} %bitcast.149, bf16[2048,3072]{1,0:T(8,128)(2,1)} %all-gather.2.cloned.1.call-done, f32[4,3072]{1,0:T(4,128)S(1)} %bitcast.157, bf16[1,128,4,3072]{3,2,1,0:T(4,128)(2,1)} %param.22), kind=kOutput, calls=%fused_computation.104 | convolution fusion | flops 6448741888 | bytes 24168448 | tf_op jit(solution)/shard_map/dot_general | solution.py:134
  379.6 3.0 convolution_add_fusion.2
  383.7 7.1 %collective-permute-done = f32[128,4,64]{2,1,0:T(4,128)S(1)} collective-permute-done((f32[128,4,64]{2,1,0:T(4,128)S(1)}, f32[128,4,64]{2,1,0:T(4,128)S(1)}, u32[]{:S(2)}, u32[]{:S(2)}) %collective-permute-start) | collective-permute-done | bytes 131104 | tf_op jit(solution)/shard_map/ppermute | solution.py:15
  (245 shorter events, 151.7 us)
Async XLA Ops:
  7.2 372.5 %copy-start = (bf16[3072,64]{0,1:T(8,128)(2,1)S(1)}, bf16[3072,64]{0,1:T(8,128)(2,1)}, u32[]{:S(2)}) copy-start(bf16[3072,64]{0,1:T(8,128)(2,1)} %param.36) | copy-start | bytes 1179652
  9.2 22.4 %all-to-all-start.2 = ((bf16[16,64,128]{2,0,1:T(8,128)(2,1)}), bf16[16,64,128]{2,0,1:T(8,128)(2,1)S(1)}, u32[]{:S(2)}, u32[]{:S(2)}) async-start(bf16[16,64,128]{2,0,1:T(8,128)(2,1)} %copy.81), calls=%async_computation.2 | async-start | bytes 524288 | tf_op jit(solution)/shard_map/all_to_all | solution.py:110
  27.8 2.5 copy-start.8
  31.6 7.4 %copy-start.4 = (bf16[16,64,128]{2,0,1:T(8,128)(2,1)}, bf16[16,64,128]{2,0,1:T(8,128)(2,1)S(1)}, u32[]{:S(2)}) copy-start(bf16[16,64,128]{2,0,1:T(8,128)(2,1)S(1)} %all-to-all-done.2) | copy-start | bytes 786436
  31.6 16.3 %all-to-all-start.4 = ((bf16[16,64,128]{2,0,1:T(8,128)(2,1)}), bf16[16,64,128]{2,0,1:T(8,128)(2,1)S(1)}, u32[]{:S(2)}, u32[]{:S(2)}) async-start(bf16[16,64,128]{2,0,1:T(8,128)(2,1)} %copy.86), calls=%async_computation.4 | async-start | bytes 524288 | tf_op jit(solution)/shard_map/all_to_all | solution.py:111
  48.7 34.7 %all-to-all-start.1 = ((bf16[128,64,128]{0,2,1:T(8,128)(2,1)}), bf16[128,64,128]{0,2,1:T(8,128)(2,1)S(1)}, u32[]{:S(2)}, u32[]{:S(2)}) async-start(bf16[128,64,128]{0,2,1:T(8,128)(2,1)} %pad_maximum_fusion.1), calls=%async_computation.1 | async-start | bytes 4194304 | tf_op jit(solution)/shard_map/all_to_all | solution.py:108
  83.4 33.6 %all-to-all-start.3 = ((bf16[128,64,128]{0,2,1:T(8,128)(2,1)}), bf16[128,64,128]{0,2,1:T(8,128)(2,1)}, u32[]{:S(2)}, u32[]{:S(2)}) async-start(bf16[128,64,128]{0,2,1:T(8,128)(2,1)} %bitcast.141), calls=%async_computation.3 | async-start | bytes 4194304 | tf_op jit(solution)/shard_map/all_to_all | solution.py:109
  88.1 34.4 %copy-start.15 = (s32[1,4]{1,0:T(1,128)S(1)}, s32[1,4]{1,0:T(1,128)}, u32[]{:S(2)}) copy-start(s32[1,4]{1,0:T(1,128)} %param.28) | copy-start | bytes 52
  90.9 32.3 %copy-start.5 = (bf16[16,64,128]{2,0,1:T(8,128)(2,1)S(1)}, bf16[16,64,128]{2,0,1:T(8,128)(2,1)}, u32[]{:S(2)}) copy-start(bf16[16,64,128]{2,0,1:T(8,128)(2,1)} %copy-done.4) | copy-start | bytes 786436
  90.9 32.4 %copy-start.7 = (bf16[16,64,128]{2,0,1:T(8,128)(2,1)S(1)}, bf16[16,64,128]{2,0,1:T(8,128)(2,1)}, u32[]{:S(2)}) copy-start(bf16[16,64,128]{2,0,1:T(8,128)(2,1)} %copy-done.6) | copy-start | bytes 786436
  117.0 38.5 %all-to-all-start = ((bf16[128,64,128]{0,2,1:T(8,128)(2,1)}), bf16[128,64,128]{0,2,1:T(8,128)(2,1)}, u32[]{:S(2)}, u32[]{:S(2)}) async-start(bf16[128,64,128]{0,2,1:T(8,128)(2,1)} %pad_maximum_fusion), calls=%async_computation | async-start | bytes 4194304 | tf_op jit(solution)/shard_map/all_to_all | solution.py:107
  121.8 238.7 %all-gather.2.cloned.1.call-start = ((), (), s32[]{:S(2)}) async-start(), calls=%async_computation.6 | async-start | bytes 12779520 | tf_op jit(solution)/shard_map/all_gather | solution.py:136
  158.7 2.4 copy-start.1
  158.7 3.0 copy-start.2
  224.5 1.5 copy-start.10
  233.5 1.5 copy-start.10
  242.5 1.5 copy-start.9
  258.5 1.5 copy-start.9
  266.5 1.5 copy-start.9
  274.4 1.5 copy-start.9
  282.4 1.5 copy-start.9
  290.4 1.5 copy-start.9
  298.4 1.5 copy-start.9
  301.9 25.1 %copy-start.11 = (f32[128,4,32]{0,2,1:T(8,128)S(1)}, f32[128,4,32]{0,2,1:T(8,128)}, u32[]{:S(2)}) copy-start(f32[128,4,32]{0,2,1:T(8,128)} %param.21) | copy-start | bytes 196612
  301.9 26.0 %copy-start.13 = (f32[1,4,3072]{2,1,0:T(4,128)S(1)}, f32[1,4,3072]{2,1,0:T(4,128)}, u32[]{:S(2)}) copy-start(f32[1,4,3072]{2,1,0:T(4,128)} %param.35) | copy-start | bytes 147460
  320.0 35.7 %all-to-all-start.5 = ((bf16[4096,2,128]{2,1,0:T(2,128)(2,1)}), bf16[4096,2,128]{2,1,0:T(2,128)(2,1)S(1)}, u32[]{:S(2)}, u32[]{:S(2)}) async-start(bf16[4096,2,128]{2,1,0:T(2,128)(2,1)} %copy.88), calls=%async_computation.5 | async-start | bytes 4194304 | tf_op jit(solution)/shard_map/all_to_all | solution.py:132
  327.9 32.6 %copy-start.18 = (f32[1,4,3072]{2,1,0:T(4,128)S(1)}, f32[1,4,3072]{2,1,0:T(4,128)}, u32[]{:S(2)}) copy-start(f32[1,4,3072]{2,1,0:T(4,128)} %param.33) | copy-start | bytes 147460
  377.1 2.5 copy-start.14
  377.2 6.5 %copy-start.16 = (s32[4]{0:T(128)S(1)}, s32[4]{0:T(128)}, u32[]{:S(2)}) copy-start(s32[4]{0:T(128)} %param.30) | copy-start | bytes 52
  377.2 6.5 %copy-start.17 = (s32[4]{0:T(128)S(1)}, s32[4]{0:T(128)}, u32[]{:S(2)}) copy-start(s32[4]{0:T(128)} %param.31) | copy-start | bytes 52
  379.6 11.1 %copy-start.3 = (f32[128,4,32]{2,1,0:T(4,128)S(1)}, f32[128,4,32]{2,1,0:T(4,128)}, u32[]{:S(2)}) copy-start(f32[128,4,32]{2,1,0:T(4,128)} %copy.94) | copy-start | bytes 196612
  382.8 8.0 %collective-permute-start = (f32[128,4,64]{2,1,0:T(4,128)S(1)}, f32[128,4,64]{2,1,0:T(4,128)S(1)}, u32[]{:S(2)}, u32[]{:S(2)}) collective-permute-start(f32[128,4,64]{2,1,0:T(4,128)S(1)} %bitcast.150), channel_id=1, source_target_pairs={{0,64},{64,0},{1,65},{65,1},{2,66},{66,2},{3,67},{67,3},{4,68},{68... | collective-permute-start | bytes 393224 | tf_op jit(solution)/shard_map/ppermute | solution.py:15
  (9 other events, 12.0 us)
Sparse Core Ops, SparseCore 0:
  124.3 124.6 all-gather.1
where the time goes:
time: 402 us; the launch traced here: 399 us
  waiting for transfers between devices  112 us (28%)
  matrix products  112 us (28%)
  local copies, waits for them, and re-layouts  62.2 us (15%)
  other arithmetic  59 us (15%)
  starting transfers between devices  39.1 us (10%)
  between operations  14.4 us (4%)
    dot_general x16, matrix products, attend(): jnp.dot(queries, keys_img.T, preferred_element_type=jnp.float32) * factor  39.2 us
    all_to_all x1, waiting for transfers between devices, shards(): lax.all_to_all(attended, 'seq', split_axis=0, concat_axis=1, tiled=True)  27.8 us
    reduce_sum x32, other arithmetic, attend(): total = jnp.sum(exp_img, axis=1) + jnp.sum(exp_txt, axis=1)  27.5 us
    all_to_all x1, waiting for transfers between devices, shards(): lax.all_to_all(vals, 'seq', split_axis=1, concat_axis=0, tiled=True)  26.1 us
    all_to_all x1, waiting for transfers between devices, shards(): lax.all_to_all(rot_key, 'seq', split_axis=1, concat_axis=0, tiled=True)  24.4 us
    all_to_all x1, waiting for transfers between devices, shards(): lax.all_to_all(rot_query, 'seq', split_axis=1, concat_axis=0, tiled=True)  24.4 us
    dot_general x16, matrix products, attend(): jnp.dot(exp_img.astype(jnp.bfloat16), values_img, preferred_element_type=...  23.6 us
    dot_general x16, matrix products, attend(): jnp.dot(queries, keys_txt.T, preferred_element_type=jnp.float32) * factor  20.6 us
  transfers between devices with their start and end apart: 8, of which 6 were waited for; matrix products, arithmetic and copies ran while one was open for 51% of the time, Pallas kernels for 0%

commit v1 on v0

--- a/solution.py
+++ b/solution.py
@@ -1,12 +1,17 @@
+import functools
 import math
 
 import jax
 import jax.numpy as jnp
 from jax import lax
+from jax.experimental import pallas as pl
+from jax.experimental.pallas import tpu as pltpu
 from jax.sharding import PartitionSpec as P
 
 HSIZE = 128
 STEPS = 28
+QBLOCK = 512
+KBLOCK = 512
 
 
 def partner_2(value, axis, distance):
@@ -36,32 +41,82 @@
     )
 
 
-def attend(queries, keys_img, values_img, keys_txt, values_txt, length):
+def attend_kernel(lens_ref, q_ref, k_ref, v_ref, kt_ref, vt_ref, o_ref, s_scr, acc_scr, l_scr):
+    member = pl.program_id(0)
+    length = lens_ref[member]
     factor = HSIZE ** (-0.5)
-    score_img = jnp.dot(queries, keys_img.T, preferred_element_type=jnp.float32) * factor
-    score_txt = jnp.dot(queries, keys_txt.T, preferred_element_type=jnp.float32) * factor
-    live = jnp.arange(keys_txt.shape[0], dtype=jnp.int32) < length
-    score_txt = jnp.where(live[None, :], score_txt, jnp.float32(-1e30))
-    top = jnp.maximum(jnp.max(score_img, axis=1), jnp.max(score_txt, axis=1))
-    exp_img = jnp.exp(score_img - top[:, None])
-    exp_txt = jnp.where(live[None, :], jnp.exp(score_txt - top[:, None]), jnp.float32(0.0))
-    total = jnp.sum(exp_img, axis=1) + jnp.sum(exp_txt, axis=1)
-    summed = jnp.dot(exp_img.astype(jnp.bfloat16), values_img, preferred_element_type=jnp.float32)
-    summed = summed + jnp.dot(
-        exp_txt.astype(jnp.bfloat16), values_txt, preferred_element_type=jnp.float32
-    )
-    return (summed / total[:, None]).astype(jnp.bfloat16)
-
-
-def attend_blocks(queries, keys_img, values_img, keys_txt, values_txt, length):
-    query_rows = queries.shape[0]
-    block_rows = math.gcd(query_rows, 512)
-    blocked = queries.reshape(query_rows // block_rows, block_rows, queries.shape[1])
-
-    def one_block(block):
-        return attend(block, keys_img, values_img, keys_txt, values_txt, length)
-
-    return lax.map(one_block, blocked).reshape(query_rows, queries.shape[1])
+    q = q_ref[...]
+    rows = q.shape[0]
+    n_keys = k_ref.shape[0]
+    n_chunks = n_keys // KBLOCK
+    dims = (((1,), (1,)), ((), ()))
+
+    def scores(c, top):
+        start = pl.multiple_of(c * KBLOCK, KBLOCK)
+        s = lax.dot_general(q, k_ref[pl.ds(start, KBLOCK), :], dims,
+                            preferred_element_type=jnp.float32) * factor
+        s_scr[:, pl.ds(start, KBLOCK)] = s
+        return jnp.maximum(top, jnp.max(s, axis=1, keepdims=True))
+
+    top = lax.fori_loop(0, n_chunks, scores,
+                        jnp.full((rows, 1), -jnp.inf, jnp.float32))
+    st = lax.dot_general(q, kt_ref[...], dims, preferred_element_type=jnp.float32) * factor
+    live = lax.broadcasted_iota(jnp.int32, st.shape, 1) < length
+    st = jnp.where(live, st, jnp.float32(-1e30))
+    top = jnp.maximum(top, jnp.max(st, axis=1, keepdims=True))
+    pt = jnp.where(live, jnp.exp(st - top), jnp.float32(0.0))
+    l_scr[...] = jnp.sum(pt, axis=1, keepdims=True)
+    acc_scr[...] = jnp.dot(pt.astype(jnp.bfloat16), vt_ref[...],
+                           preferred_element_type=jnp.float32)
+
+    def weigh(c, carry):
+        start = pl.multiple_of(c * KBLOCK, KBLOCK)
+        p = jnp.exp(s_scr[:, pl.ds(start, KBLOCK)] - top)
+        l_scr[...] += jnp.sum(p, axis=1, keepdims=True)
+        acc_scr[...] += jnp.dot(p.astype(jnp.bfloat16), v_ref[pl.ds(start, KBLOCK), :],
+                                preferred_element_type=jnp.float32)
+        return carry
+
+    lax.fori_loop(0, n_chunks, weigh, 0)
+    o_ref[...] = (acc_scr[...] / l_scr[...]).astype(o_ref.dtype)
+
+
+def attend_members(qkv, text_kv, lengths):
+    members, img = qkv.shape[1], qkv.shape[2]
+    txt = text_kv.shape[2]
+    nq = img // QBLOCK
+    grid_spec = pltpu.PrefetchScalarGridSpec(
+        num_scalar_prefetch=1,
+        grid=(members, nq),
+        in_specs=[
+            pl.BlockSpec((None, None, QBLOCK, HSIZE), lambda m, i, lens: (0, m, i, 0)),
+            pl.BlockSpec((None, None, img, HSIZE), lambda m, i, lens: (1, m, 0, 0)),
+            pl.BlockSpec((None, None, img, HSIZE), lambda m, i, lens: (2, m, 0, 0)),
+            pl.BlockSpec((None, None, txt, HSIZE), lambda m, i, lens: (0, m, 0, 0)),
+            pl.BlockSpec((None, None, txt, HSIZE), lambda m, i, lens: (1, m, 0, 0)),
+        ],
+        out_specs=pl.BlockSpec((None, QBLOCK, HSIZE), lambda m, i, lens: (m, i, 0)),
+        scratch_shapes=[
+            pltpu.VMEM((QBLOCK, img), jnp.float32),
+            pltpu.VMEM((QBLOCK, HSIZE), jnp.float32),
+            pltpu.VMEM((QBLOCK, 1), jnp.float32),
+        ],
+    )
+    flops = members * img * (img + txt) * HSIZE * 4
+    return pl.pallas_call(
+        attend_kernel,
+        grid_spec=grid_spec,
+        out_shape=jax.ShapeDtypeStruct((members, img, HSIZE), jnp.bfloat16),
+        compiler_params=pltpu.CompilerParams(
+            dimension_semantics=("arbitrary", "arbitrary"),
+            vmem_limit_bytes=48 * 1024 * 1024,
+        ),
+        cost_estimate=pl.CostEstimate(
+            flops=flops,
+            transcendentals=members * img * (img + txt),
+            bytes_accessed=members * (img * 4 + txt * 2) * HSIZE * 2,
+        ),
+    )(lengths, qkv, qkv, qkv, text_kv, text_kv)
 
 
 def roster(fraction):
@@ -93,6 +148,8 @@
     head_count = feature_width // HSIZE
     text_rows = key_txt.shape[1]
     members = prompt_count * head_count
+    groups = lax.axis_size("seq")
+    held = members // groups
     angle = rope_angles(img_ids)[:, None, :]
     rot_query = rotate(
         query_img[0].reshape(img_rows, members, HSIZE).astype(jnp.float32), angle
@@ -101,35 +158,25 @@
         key_img[0].reshape(img_rows, members, HSIZE).astype(jnp.float32), angle
     ).astype(jnp.bfloat16)
     vals = value_img[0].reshape(img_rows, members, HSIZE)
-    text_keys = key_txt[0].reshape(text_rows, members, HSIZE)
-    text_vals = value_txt[0].reshape(text_rows, members, HSIZE)
-    all_query, all_key, all_vals, all_text_keys, all_text_vals = (
-        lax.all_to_all(rot_query, "seq", split_axis=1, concat_axis=0, tiled=True),
-        lax.all_to_all(rot_key, "seq", split_axis=1, concat_axis=0, tiled=True),
-        lax.all_to_all(vals, "seq", split_axis=1, concat_axis=0, tiled=True),
-        lax.all_to_all(text_keys, "seq", split_axis=1, concat_axis=0, tiled=True),
-        lax.all_to_all(text_vals, "seq", split_axis=1, concat_axis=0, tiled=True),
-    )
-    held = all_query.shape[1]
+    stacked = jnp.stack([rot_query, rot_key, vals])
+    stacked = stacked.reshape(3, img_rows, groups, held, HSIZE).transpose(2, 0, 3, 1, 4)
+    text_stacked = jnp.stack(
+        [key_txt[0].reshape(text_rows, members, HSIZE), value_txt[0].reshape(text_rows, members, HSIZE)]
+    )
+    text_stacked = text_stacked.reshape(2, text_rows, groups, held, HSIZE).transpose(2, 0, 3, 1, 4)
+    got = lax.all_to_all(stacked, "seq", 0, 0, tiled=True)
+    got_text = lax.all_to_all(text_stacked, "seq", 0, 0, tiled=True)
+    got = got.reshape(groups, 3, held, img_rows, HSIZE).transpose(1, 2, 0, 3, 4)
+    got = got.reshape(3, held, groups * img_rows, HSIZE)
+    got_text = got_text.reshape(groups, 2, held, text_rows, HSIZE).transpose(1, 2, 0, 3, 4)
+    got_text = got_text.reshape(2, held, groups * text_rows, HSIZE)
     first_member = lax.axis_index("seq") * held
-    lengths = text_len[0]
-    prompt_slots = jnp.arange(prompt_count, dtype=jnp.int32)
-    results = []
-    for member in range(held):
-        prompt_of = (first_member + member) // head_count
-        length = jnp.sum(jnp.where(prompt_slots == prompt_of, lengths, 0))
-        results.append(
-            attend_blocks(
-                all_query[:, member],
-                all_key[:, member],
-                all_vals[:, member],
-                all_text_keys[:, member],
-                all_text_vals[:, member],
-                length,
-            )
-        )
-    attended = jnp.stack(results, axis=1)
-    returned = lax.all_to_all(attended, "seq", split_axis=0, concat_axis=1, tiled=True)
+    member_ids = first_member + jnp.arange(held, dtype=jnp.int32)
+    lengths = jnp.take(text_len[0], member_ids // head_count)
+    attended = attend_members(got, got_text, lengths)
+    attended = attended.reshape(held, groups, img_rows, HSIZE).transpose(1, 0, 2, 3)
+    returned = lax.all_to_all(attended, "seq", 0, 0, tiled=True)
+    returned = returned.reshape(members, img_rows, HSIZE).transpose(1, 0, 2)
     flat_attended = returned.reshape(img_rows * prompt_count, feature_width)
     projected = jnp.dot(
         flat_attended,

time: 402 us -> 356 us (0.89)
  Pallas kernels: 0 us -> 109 us
  matrix products: 112 us -> 15.3 us
  other arithmetic: 59 us -> 9.57 us
  local copies, waits for them, and re-layouts: 62.2 us -> 40.8 us
  waiting for transfers between devices: 112 us -> 131 us
    pallas_call x0 -> x1, Pallas kernels: none -> 109 us  [attend_members(): pl.pallas_call(attend_kernel, grid_spec=grid_spec, out_shape=jax.ShapeDty...]
    dot_general x64 -> x0, matrix products: 97.2 us -> none  [the longest x16 39.2 us: attend(): jnp.dot(queries, keys_img.T, preferred_element_type=jnp.float32) * factor]
    reduce_sum x33 -> x0, other arithmetic: 28.1 us -> none  [the longest x32 27.5 us: attend(): total = jnp.sum(exp_img, axis=1) + jnp.sum(exp_txt, axis=1)]
    another operation x7 -> x2, local copies, waits for them, and re-layouts: 22.5 us -> 2.24 us  [shards(): jnp.stack([key_txt[0].reshape(text_rows, members, HSIZE), value_txt[0].re...]
    all_to_all x6 -> x3, waiting for transfers between devices: 104 us -> 122 us  [the longest x1 94.1 us: shards(): got = lax.all_to_all(stacked, 'seq', 0, 0, tiled=True)]
    transpose x0 -> x5, local copies, waits for them, and re-layouts: none -> 17.2 us  [the longest x1 8.75 us: shards(): got = got.reshape(groups, 3, held, img_rows, HSIZE).transpose(1, 2, 0, 3, 4)]
    all_to_all x7 -> x0, local copies, waits for them, and re-layouts: 15.1 us -> none  [the longest x2 4.84 us: shards(): lax.all_to_all(attended, 'seq', split_axis=0, concat_axis=1, tiled=True)]
    lt x16 -> x0, other arithmetic: 10.3 us -> none  [attend(): live = jnp.arange(keys_txt.shape[0], dtype=jnp.int32) < length]
  transfers between devices with their start and end apart: 8 -> 5, of which waited for: 6 -> 3; matrix products, arithmetic and copies ran while one was open for 51% -> 12% of each run, Pallas kernels for 0% -> 31%
where the time goes in v1:
time: 356 us; the launch traced here: 355 us
  waiting for transfers between devices  131 us (37%)
  Pallas kernels  109 us (31%)
  local copies, waits for them, and re-layouts  40.8 us (11%)
  starting transfers between devices  35.5 us (10%)
  matrix products  15.3 us (4%)
  between operations  14.3 us (4%)
  other arithmetic  9.57 us (3%)
    pallas_call x1, Pallas kernels, attend_members(): pl.pallas_call(attend_kernel, grid_spec=grid_spec, out_shape=jax.ShapeDty...  109 us
    all_to_all x1, waiting for transfers between devices, shards(): got = lax.all_to_all(stacked, 'seq', 0, 0, tiled=True)  94.1 us
    all_to_all x1, waiting for transfers between devices, shards(): returned = lax.all_to_all(attended, 'seq', 0, 0, tiled=True)  27.9 us
    all_to_all x1, starting transfers between devices, shards(): returned = lax.all_to_all(attended, 'seq', 0, 0, tiled=True)  19.4 us
    dot_general x1, matrix products, shards(): jnp.dot(flat_attended, lax.all_gather(proj_weight, ('cfg', 'seq'), axis=0...  12.3 us
    transpose x1, local copies, waits for them, and re-layouts, shards(): got = got.reshape(groups, 3, held, img_rows, HSIZE).transpose(1, 2, 0, 3, 4)  8.75 us
    all_to_all x1, starting transfers between devices, shards(): got_text = lax.all_to_all(text_stacked, 'seq', 0, 0, tiled=True)  8.33 us
    ppermute x1, waiting for transfers between devices, partner_2(): return lax.ppermute(value, axis, pairs)  7.85 us
  transfers between devices with their start and end apart: 5, of which 3 were waited for; matrix products, arithmetic and copies ran while one was open for 12% of the time, Pallas kernels for 31%

profile of v1, /device:TPU:6, one launch (start us, length us, event | category | flops | bytes accessed | tf_op | source)
XLA Modules:
  0.0 354.8 jit_solution(4269140566634421340)
XLA Ops:
  7.2 0.7 all-gather.2.cloned.1.call-update
  7.9 1.1 stack.16
  9.0 1.1 stack.17
  10.2 0.7 maximum_bitcast_fusion.1
  10.9 1.5 copy.64
  12.4 8.3 %all-to-all-start.1 = ((bf16[32,2,2,16,128]{4,3,2,1,0:T(8,128)(2,1)}), bf16[32,2,2,16,128]{4,3,2,1,0:T(8,128)(2,1)S(1)}, u32[]{:S(2)}, u32[]{:S(2)}) async-start(bf16[32,2,2,16,128]{4,3,2,1,0:T(8,128)(2,1)} %copy.64), calls=%async_computation.1 | async-start | bytes 1048576 | tf_op jit(solution)/shard_map/all_to_all | solution.py:168
  20.7 3.4 copy.60
  24.2 4.9 %copy.59 = f32[1,128,4,2048]{1,3,2,0:T(8,128)} copy(bf16[1,128,4,2048]{3,2,1,0:T(4,128)(2,1)} %param.19) | data formatting | bytes 6291456 | tf_op jit(solution)/shard_map/convert_element_type | solution.py:155
  29.1 3.4 copy.61
  32.9 4.8 %subtract_convert_fusion.1 = (bf16[128,64,64]{0,2,1:T(8,128)(2,1)S(1)}, bf16[128,64,64]{0,2,1:T(8,128)(2,1)S(1)}, bf16[128,64,64]{0,2,1:T(8,128)(2,1)S(1)}, bf16[128,64,64]{0,2,1:T(8,128)(2,1)S(1)}) fusion(f32[128,64,128]{0,2,1:T(8,128)} %bitcast.55, f32[128,64]{0,1:T(8,128)S(1)} %get-tuple-element.19, f32[128,64]{0,1:T(8,128)S(1)} %get-tuple-element.18, ...), kind=kLoop, calls=%fused_computation.11 | loop fusion | flops 8388608 | bytes 12648448 | tf_op jit(solution)/shard_map/convert.10
  37.7 0.8 maximum_bitcast_fusion
  38.5 4.0 %copy.62 = bf16[32,3,2,128,128]{3,4,2,1,0:T(8,128)(2,1)} copy(bf16[32,3,2,128,128]{3,4,2,0,1:T(8,128)(2,1)S(1)} %maximum_bitcast_fusion) | data formatting | bytes 12582912 | tf_op jit(solution)/shard_map/transpose | solution.py:162
  42.5 7.6 %all-to-all-start = ((bf16[32,3,2,128,128]{3,4,2,1,0:T(8,128)(2,1)}), bf16[32,3,2,128,128]{3,4,2,1,0:T(8,128)(2,1)}, u32[]{:S(2)}, u32[]{:S(2)}) async-start(bf16[32,3,2,128,128]{3,4,2,1,0:T(8,128)(2,1)} %copy.62), calls=%async_computation | async-start | bytes 12582912 | tf_op jit(solution)/shard_map/all_to_all | solution.py:167
  50.2 0.6 gather_fusion
  50.9 94.1 %all-to-all-done = bf16[32,3,2,128,128]{3,4,2,1,0:T(8,128)(2,1)} async-done(((bf16[32,3,2,128,128]{3,4,2,1,0:T(8,128)(2,1)}), bf16[32,3,2,128,128]{3,4,2,1,0:T(8,128)(2,1)}, u32[]{:S(2)}, u32[]{:S(2)}) %all-to-all-start) | async-done | bytes 6291488 | tf_op jit(solution)/shard_map/all_to_all | solution.py:167
  145.0 8.8 %copy.63 = bf16[3,2,32,128,128]{4,3,2,1,0:T(8,128)(2,1)} copy(bf16[3,2,32,128,128]{3,4,1,0,2:T(8,128)(2,1)} %bitcast.15) | data formatting | bytes 12582912 | tf_op jit(solution)/shard_map/transpose | solution.py:169
  153.8 108.9 %shard_map.176 = bf16[2,4096,128]{2,1,0:T(8,128)(2,1)S(1)} custom-call(s32[2]{0:T(128)S(1)} %and_select_fusion.1.lens_ref, bf16[3,2,4096,128]{3,2,1,0:T(8,128)(2,1)} %bitcast.59, bf16[3,2,4096,128]{3,2,1,0:T(8,128)(2,1)} %bitcast.60, bf16[3,2,4096,128]{3,2,1,0:T(8,128)(2,1)} %bitcast.61, bf16[2,2,512,128]{3,2,1,0:T(8,128)(2,1)S(1)} %bitcast.51, ...), custom_call_target="tpu_custom_call" | custom-call | flops 19327352832 | bytes 8912896 | tf_op jit(solution)/shard_map/pallas_call | solution.py:106
  262.8 1.6 copy.78
  264.3 19.4 %all-to-all-start.2 = ((bf16[32,2,128,128]{3,2,1,0:T(8,128)(2,1)}), bf16[32,2,128,128]{3,2,1,0:T(8,128)(2,1)S(1)}, u32[]{:S(2)}, u32[]{:S(2)}) async-start(bf16[32,2,128,128]{3,2,1,0:T(8,128)(2,1)} %bitcast.57), calls=%async_computation.2 | async-start | bytes 4194304 | tf_op jit(solution)/shard_map/all_to_all | solution.py:178
  283.7 0.9 copy.71
  284.6 27.9 %all-to-all-done.2 = bf16[32,2,128,128]{3,2,1,0:T(8,128)(2,1)S(1)} async-done(((bf16[32,2,128,128]{3,2,1,0:T(8,128)(2,1)}), bf16[32,2,128,128]{3,2,1,0:T(8,128)(2,1)S(1)}, u32[]{:S(2)}, u32[]{:S(2)}) %all-to-all-start.2) | async-done | bytes 2097184 | tf_op jit(solution)/shard_map/all_to_all | solution.py:178
  312.5 2.9 copy.67
  315.4 12.3 %fusion.7 = (f32[128,4]{0,1:T(4,128)S(1)}, f32[128,4,3072]{2,0,1:T(8,128)S(1)}) fusion(bf16[128,4,2048]{0,2,1:T(8,128)(2,1)} %bitcast.66, bf16[2048,3072]{1,0:T(8,128)(2,1)} %all-gather.2.cloned.1.call-done, f32[4,3072]{1,0:T(4,128)S(1)} %bitcast.71, bf16[1,128,4,3072]{3,2,1,0:T(4,128)(2,1)} %param.18), kind=kOutput, calls=%fused_computation.47 | convolution fusion | flops 6448741888 | bytes 24168448 | tf_op jit(solution)/shard_map/dot_general | solution.py:181
  327.7 0.8 multiply_reduce_fusion
  328.4 1.7 add_convert_fusion
  330.1 2.4 copy.69
  332.6 2.4 reshape.309
  335.0 3.0 convolution_add_fusion
  338.3 7.8 %collective-permute-done = f32[128,4,64]{2,1,0:T(4,128)S(1)} collective-permute-done((f32[128,4,64]{2,1,0:T(4,128)S(1)}, f32[128,4,64]{2,1,0:T(4,128)S(1)}, u32[]{:S(2)}, u32[]{:S(2)}) %collective-permute-start) | collective-permute-done | bytes 131104 | tf_op jit(solution)/shard_map/ppermute | solution.py:20
  346.2 0.3 multiply_subtract_fusion
  346.5 0.7 copy.73
  347.3 0.7 copy.74
  (43 shorter events, 0.7 us)
Async XLA Ops:
  7.2 327.9 %copy-start = (bf16[3072,64]{0,1:T(8,128)(2,1)S(1)}, bf16[3072,64]{0,1:T(8,128)(2,1)}, u32[]{:S(2)}) copy-start(bf16[3072,64]{0,1:T(8,128)(2,1)} %param.32) | copy-start | bytes 1179652
  7.2 13.5 %copy-start.2 = (bf16[1,128,4,2048]{3,2,1,0:T(4,128)(2,1)S(1)}, bf16[1,128,4,2048]{3,2,1,0:T(4,128)(2,1)}, u32[]{:S(2)}) copy-start(bf16[1,128,4,2048]{3,2,1,0:T(4,128)(2,1)} %param.20) | copy-start | bytes 6291460
  7.2 308.2 %all-gather.2.cloned.1.call-start = ((), (), s32[]{:S(2)}) async-start(), calls=%async_computation.3 | async-start | bytes 12779520 | tf_op jit(solution)/shard_map/all_gather | solution.py:183
  12.4 30.2 %all-to-all-start.1 = ((bf16[32,2,2,16,128]{4,3,2,1,0:T(8,128)(2,1)}), bf16[32,2,2,16,128]{4,3,2,1,0:T(8,128)(2,1)S(1)}, u32[]{:S(2)}, u32[]{:S(2)}) async-start(bf16[32,2,2,16,128]{4,3,2,1,0:T(8,128)(2,1)} %copy.64), calls=%async_computation.1 | async-start | bytes 1048576 | tf_op jit(solution)/shard_map/all_to_all | solution.py:168
  24.2 8.4 %copy-start.8 = (s32[3,128]{1,0:T(4,128)S(1)}, s32[3,128]{1,0:T(4,128)}, u32[]{:S(2)}) copy-start(s32[3,128]{1,0:T(4,128)} %param.25) | copy-start | bytes 4612
  42.5 7.7 %copy-start.1 = (s32[1,4]{1,0:T(1,128)S(1)}, s32[1,4]{1,0:T(1,128)}, u32[]{:S(2)}) copy-start(s32[1,4]{1,0:T(1,128)} %param.24) | copy-start | bytes 52
  42.5 102.5 %all-to-all-start = ((bf16[32,3,2,128,128]{3,4,2,1,0:T(8,128)(2,1)}), bf16[32,3,2,128,128]{3,4,2,1,0:T(8,128)(2,1)}, u32[]{:S(2)}, u32[]{:S(2)}) async-start(bf16[32,3,2,128,128]{3,4,2,1,0:T(8,128)(2,1)} %copy.62), calls=%async_computation | async-start | bytes 12582912 | tf_op jit(solution)/shard_map/all_to_all | solution.py:167
  262.7 21.0 %copy-start.4 = (f32[128,4,32]{0,2,1:T(8,128)S(1)}, f32[128,4,32]{0,2,1:T(8,128)}, u32[]{:S(2)}) copy-start(f32[128,4,32]{0,2,1:T(8,128)} %param.17) | copy-start | bytes 196612
  262.7 21.8 %copy-start.6 = (f32[1,4,3072]{2,1,0:T(4,128)S(1)}, f32[1,4,3072]{2,1,0:T(4,128)}, u32[]{:S(2)}) copy-start(f32[1,4,3072]{2,1,0:T(4,128)} %param.31) | copy-start | bytes 147460
  264.3 51.1 %copy-start.11 = (f32[1,4,3072]{2,1,0:T(4,128)S(1)}, f32[1,4,3072]{2,1,0:T(4,128)}, u32[]{:S(2)}) copy-start(f32[1,4,3072]{2,1,0:T(4,128)} %param.29) | copy-start | bytes 147460
  264.3 48.1 %all-to-all-start.2 = ((bf16[32,2,128,128]{3,2,1,0:T(8,128)(2,1)}), bf16[32,2,128,128]{3,2,1,0:T(8,128)(2,1)S(1)}, u32[]{:S(2)}, u32[]{:S(2)}) async-start(bf16[32,2,128,128]{3,2,1,0:T(8,128)(2,1)} %bitcast.57), calls=%async_computation.2 | async-start | bytes 4194304 | tf_op jit(solution)/shard_map/all_to_all | solution.py:178
  327.6 0.8 copy-start.5
  332.6 2.5 copy-start.7
  332.6 5.7 %copy-start.9 = (s32[4]{0:T(128)S(1)}, s32[4]{0:T(128)}, u32[]{:S(2)}) copy-start(s32[4]{0:T(128)} %param.26) | copy-start | bytes 52
  332.6 5.7 %copy-start.10 = (s32[4]{0:T(128)S(1)}, s32[4]{0:T(128)}, u32[]{:S(2)}) copy-start(s32[4]{0:T(128)} %param.27) | copy-start | bytes 52
  335.0 11.1 %copy-start.3 = (f32[128,4,32]{2,1,0:T(4,128)S(1)}, f32[128,4,32]{2,1,0:T(4,128)}, u32[]{:S(2)}) copy-start(f32[128,4,32]{2,1,0:T(4,128)} %copy.71) | copy-start | bytes 196612
  338.2 8.0 %collective-permute-start = (f32[128,4,64]{2,1,0:T(4,128)S(1)}, f32[128,4,64]{2,1,0:T(4,128)S(1)}, u32[]{:S(2)}, u32[]{:S(2)}) collective-permute-start(f32[128,4,64]{2,1,0:T(4,128)S(1)} %bitcast.68), channel_id=1, source_target_pairs={{0,64},{64,0},{1,65},{65,1},{2,66},{66,2},{3,67},{67,3},{4,68},{68... | collective-permute-start | bytes 393224 | tf_op jit(solution)/shard_map/ppermute | solution.py:20
Sparse Core Ops, SparseCore 0:
  9.7 185.4 all-gather.1

commit v2 on v1

--- a/solution.py
+++ b/solution.py
@@ -1,4 +1,3 @@
-import functools
 import math
 
 import jax
@@ -41,82 +40,103 @@
     )
 
 
-def attend_kernel(lens_ref, q_ref, k_ref, v_ref, kt_ref, vt_ref, o_ref, s_scr, acc_scr, l_scr):
-    member = pl.program_id(0)
-    length = lens_ref[member]
-    factor = HSIZE ** (-0.5)
-    q = q_ref[...]
-    rows = q.shape[0]
-    n_keys = k_ref.shape[0]
-    n_chunks = n_keys // KBLOCK
+def attend_kernel(len_ref, q_ref, k_ref, v_ref, kt_ref, vt_ref, o_ref, s_scr, m_scr, l_scr, acc_scr):
+    length = len_ref[0]
+    scale = (HSIZE ** (-0.5)) * math.log2(math.e)
+    rows = QBLOCK
+    per_chunk = KBLOCK // k_ref.shape[1]
+    n_chunks = k_ref.shape[0] // per_chunk
+    lanes = 128
     dims = (((1,), (1,)), ((), ()))
-
-    def scores(c, top):
+    q = q_ref[...].reshape(rows, HSIZE)
+    m_scr[...] = jnp.full((rows, lanes), -jnp.inf, jnp.float32)
+
+    def scores(c, carry):
         start = pl.multiple_of(c * KBLOCK, KBLOCK)
-        s = lax.dot_general(q, k_ref[pl.ds(start, KBLOCK), :], dims,
-                            preferred_element_type=jnp.float32) * factor
+        keys = k_ref[pl.ds(c * per_chunk, per_chunk)].reshape(KBLOCK, HSIZE)
+        s = lax.dot_general(q, keys, dims, preferred_element_type=jnp.float32) * scale
         s_scr[:, pl.ds(start, KBLOCK)] = s
-        return jnp.maximum(top, jnp.max(s, axis=1, keepdims=True))
-
-    top = lax.fori_loop(0, n_chunks, scores,
-                        jnp.full((rows, 1), -jnp.inf, jnp.float32))
-    st = lax.dot_general(q, kt_ref[...], dims, preferred_element_type=jnp.float32) * factor
+        top = m_scr[...]
+        for j in range(KBLOCK // lanes):
+            top = jnp.maximum(top, s[:, j * lanes:(j + 1) * lanes])
+        m_scr[...] = top
+        return carry
+
+    lax.fori_loop(0, n_chunks, scores, 0)
+    text_keys = kt_ref[...].reshape(-1, HSIZE)
+    st = lax.dot_general(q, text_keys, dims, preferred_element_type=jnp.float32) * scale
     live = lax.broadcasted_iota(jnp.int32, st.shape, 1) < length
     st = jnp.where(live, st, jnp.float32(-1e30))
-    top = jnp.maximum(top, jnp.max(st, axis=1, keepdims=True))
-    pt = jnp.where(live, jnp.exp(st - top), jnp.float32(0.0))
-    l_scr[...] = jnp.sum(pt, axis=1, keepdims=True)
-    acc_scr[...] = jnp.dot(pt.astype(jnp.bfloat16), vt_ref[...],
+    top = m_scr[...]
+    for j in range(st.shape[1] // lanes):
+        top = jnp.maximum(top, st[:, j * lanes:(j + 1) * lanes])
+    top = jnp.max(top, axis=1, keepdims=True)
+    m_scr[...] = jnp.broadcast_to(top, (rows, lanes))
+    pt = jnp.where(live, jnp.exp2(st - top), jnp.float32(0.0))
+    total = pt[:, 0:lanes]
+    for j in range(1, st.shape[1] // lanes):
+        total = total + pt[:, j * lanes:(j + 1) * lanes]
+    l_scr[...] = total
+    acc_scr[...] = jnp.dot(pt.astype(jnp.bfloat16), vt_ref[...].reshape(-1, HSIZE),
                            preferred_element_type=jnp.float32)
 
     def weigh(c, carry):
         start = pl.multiple_of(c * KBLOCK, KBLOCK)
-        p = jnp.exp(s_scr[:, pl.ds(start, KBLOCK)] - top)
-        l_scr[...] += jnp.sum(p, axis=1, keepdims=True)
-        acc_scr[...] += jnp.dot(p.astype(jnp.bfloat16), v_ref[pl.ds(start, KBLOCK), :],
-                                preferred_element_type=jnp.float32)
+        tb = m_scr[...]
+        parts = [jnp.exp2(s_scr[:, pl.ds(start + j * lanes, lanes)] - tb)
+                 for j in range(KBLOCK // lanes)]
+        total = l_scr[...]
+        for part in parts:
+            total = total + part
+        l_scr[...] = total
+        p = jnp.concatenate(parts, axis=1).astype(jnp.bfloat16)
+        vals = v_ref[pl.ds(c * per_chunk, per_chunk)].reshape(KBLOCK, HSIZE)
+        acc_scr[...] += jnp.dot(p, vals, preferred_element_type=jnp.float32)
         return carry
 
     lax.fori_loop(0, n_chunks, weigh, 0)
-    o_ref[...] = (acc_scr[...] / l_scr[...]).astype(o_ref.dtype)
-
-
-def attend_members(qkv, text_kv, lengths):
-    members, img = qkv.shape[1], qkv.shape[2]
-    txt = text_kv.shape[2]
-    nq = img // QBLOCK
+    denom = jnp.sum(l_scr[...], axis=1, keepdims=True)
+    o_ref[...] = (acc_scr[...] / denom).astype(o_ref.dtype).reshape(o_ref.shape)
+
+
+def attend_member(chunk, text_chunk, length):
+    sources, tokens = chunk.shape[0], chunk.shape[2]
+    text_tokens = text_chunk.shape[2]
+    img = sources * tokens
+    txt = sources * text_tokens
+    per_block = QBLOCK // tokens
     grid_spec = pltpu.PrefetchScalarGridSpec(
         num_scalar_prefetch=1,
-        grid=(members, nq),
+        grid=(img // QBLOCK,),
         in_specs=[
-            pl.BlockSpec((None, None, QBLOCK, HSIZE), lambda m, i, lens: (0, m, i, 0)),
-            pl.BlockSpec((None, None, img, HSIZE), lambda m, i, lens: (1, m, 0, 0)),
-            pl.BlockSpec((None, None, img, HSIZE), lambda m, i, lens: (2, m, 0, 0)),
-            pl.BlockSpec((None, None, txt, HSIZE), lambda m, i, lens: (0, m, 0, 0)),
-            pl.BlockSpec((None, None, txt, HSIZE), lambda m, i, lens: (1, m, 0, 0)),
+            pl.BlockSpec((per_block, None, tokens, HSIZE), lambda i, lens: (i, 0, 0, 0)),
+            pl.BlockSpec((sources, None, tokens, HSIZE), lambda i, lens: (0, 1, 0, 0)),
+            pl.BlockSpec((sources, None, tokens, HSIZE), lambda i, lens: (0, 2, 0, 0)),
+            pl.BlockSpec((sources, None, text_tokens, HSIZE), lambda i, lens: (0, 0, 0, 0)),
+            pl.BlockSpec((sources, None, text_tokens, HSIZE), lambda i, lens: (0, 1, 0, 0)),
         ],
-        out_specs=pl.BlockSpec((None, QBLOCK, HSIZE), lambda m, i, lens: (m, i, 0)),
+        out_specs=pl.BlockSpec((per_block, tokens, HSIZE), lambda i, lens: (i, 0, 0)),
         scratch_shapes=[
             pltpu.VMEM((QBLOCK, img), jnp.float32),
+            pltpu.VMEM((QBLOCK, 128), jnp.float32),
+            pltpu.VMEM((QBLOCK, 128), jnp.float32),
             pltpu.VMEM((QBLOCK, HSIZE), jnp.float32),
-            pltpu.VMEM((QBLOCK, 1), jnp.float32),
         ],
     )
-    flops = members * img * (img + txt) * HSIZE * 4
     return pl.pallas_call(
         attend_kernel,
         grid_spec=grid_spec,
-        out_shape=jax.ShapeDtypeStruct((members, img, HSIZE), jnp.bfloat16),
+        out_shape=jax.ShapeDtypeStruct((sources, tokens, HSIZE), jnp.bfloat16),
         compiler_params=pltpu.CompilerParams(
-            dimension_semantics=("arbitrary", "arbitrary"),
+            dimension_semantics=("arbitrary",),
             vmem_limit_bytes=48 * 1024 * 1024,
         ),
         cost_estimate=pl.CostEstimate(
-            flops=flops,
-            transcendentals=members * img * (img + txt),
-            bytes_accessed=members * (img * 4 + txt * 2) * HSIZE * 2,
+            flops=img * (img + txt) * HSIZE * 4,
+            transcendentals=img * (img + txt),
+            bytes_accessed=(img * 4 + txt * 2) * HSIZE * 2,
         ),
-    )(lengths, qkv, qkv, qkv, text_kv, text_kv)
+    )(length, chunk, chunk, chunk, text_chunk, text_chunk)
 
 
 def roster(fraction):
@@ -164,19 +184,16 @@
         [key_txt[0].reshape(text_rows, members, HSIZE), value_txt[0].reshape(text_rows, members, HSIZE)]
     )
     text_stacked = text_stacked.reshape(2, text_rows, groups, held, HSIZE).transpose(2, 0, 3, 1, 4)
-    got = lax.all_to_all(stacked, "seq", 0, 0, tiled=True)
-    got_text = lax.all_to_all(text_stacked, "seq", 0, 0, tiled=True)
-    got = got.reshape(groups, 3, held, img_rows, HSIZE).transpose(1, 2, 0, 3, 4)
-    got = got.reshape(3, held, groups * img_rows, HSIZE)
-    got_text = got_text.reshape(groups, 2, held, text_rows, HSIZE).transpose(1, 2, 0, 3, 4)
-    got_text = got_text.reshape(2, held, groups * text_rows, HSIZE)
     first_member = lax.axis_index("seq") * held
-    member_ids = first_member + jnp.arange(held, dtype=jnp.int32)
-    lengths = jnp.take(text_len[0], member_ids // head_count)
-    attended = attend_members(got, got_text, lengths)
-    attended = attended.reshape(held, groups, img_rows, HSIZE).transpose(1, 0, 2, 3)
-    returned = lax.all_to_all(attended, "seq", 0, 0, tiled=True)
-    returned = returned.reshape(members, img_rows, HSIZE).transpose(1, 0, 2)
+    returned = []
+    for member in range(held):
+        got = lax.all_to_all(stacked[:, :, member], "seq", 0, 0, tiled=True)
+        got_text = lax.all_to_all(text_stacked[:, :, member], "seq", 0, 0, tiled=True)
+        prompt_of = (first_member + member) // head_count
+        length = jnp.take(text_len[0], prompt_of)[None]
+        attended = attend_member(got, got_text, length)
+        returned.append(lax.all_to_all(attended, "seq", 0, 0, tiled=True))
+    returned = jnp.stack(returned, axis=1).reshape(members, img_rows, HSIZE).transpose(1, 0, 2)
     flat_attended = returned.reshape(img_rows * prompt_count, feature_width)
     projected = jnp.dot(
         flat_attended,

time: 356 us -> 323 us (0.907)
  waiting for transfers between devices: 131 us -> 25.6 us
  blocking collectives: 0 us -> 56.9 us
  local copies, waits for them, and re-layouts: 40.8 us -> 53.4 us
  Pallas kernels: 109 us -> 97.1 us
  other arithmetic: 9.57 us -> 20.8 us
    all_to_all x3 -> x5, waiting for transfers between devices: 122 us -> 16.6 us  [the longest x2 14.3 us: shards(): returned.append(lax.all_to_all(attended, 'seq', 0, 0, tiled=True))]
    all_to_all x0 -> x1, blocking collectives: none -> 56.9 us  [shards(): got = lax.all_to_all(stacked[:, :, member], 'seq', 0, 0, tiled=True)]
    transpose x5 -> x1, local copies, waits for them, and re-layouts: 17.2 us -> 2.96 us  [shards(): jnp.stack(returned, axis=1).reshape(members, img_rows, HSIZE)]
    pallas_call x1 -> x2, Pallas kernels: 109 us -> 97.1 us  [attend_member(): pl.pallas_call(attend_kernel, grid_spec=grid_spec, out_shape=jax.ShapeDty...]
    squeeze x0 -> x2, local copies, waits for them, and re-layouts: none -> 9.2 us  [the longest x1 8.33 us: shards(): got = lax.all_to_all(stacked[:, :, member], 'seq', 0, 0, tiled=True)]
    concatenate x0 -> x4, local copies, waits for them, and re-layouts: none -> 9.09 us  [rotate(): jnp.concatenate([first * cosine - second * sine, first * sine + second *...]
    transpose x1, other arithmetic: 0.82 us -> 9.26 us  [shards(): stacked.reshape(3, img_rows, groups, held, HSIZE).transpose(2, 0, 3, 1, 4)]
    unnamed x28 -> x38, local copies, waits for them, and re-layouts: 5.86 us -> 12.5 us
  transfers between devices with their start and end apart: 5 -> 7, of which waited for: 3 -> 3; matrix products, arithmetic and copies ran while one was open for 12% -> 18% of each run, Pallas kernels for 31% -> 30%
where the time goes in v2:
time: 323 us; the launch traced here: 322 us
  Pallas kernels  97.1 us (30%)
  blocking collectives  56.9 us (18%)
  local copies, waits for them, and re-layouts  53.4 us (17%)
  starting transfers between devices  36.9 us (11%)
  waiting for transfers between devices  25.6 us (8%)
  other arithmetic  20.8 us (6%)
  between operations  15.7 us (5%)
  matrix products  15.3 us (5%)
    pallas_call x2, Pallas kernels, attend_member(): pl.pallas_call(attend_kernel, grid_spec=grid_spec, out_shape=jax.ShapeDty...  97.1 us
    all_to_all x1, blocking collectives, shards(): got = lax.all_to_all(stacked[:, :, member], 'seq', 0, 0, tiled=True)  56.9 us
    all_to_all x2, starting transfers between devices, shards(): lax.all_to_all(text_stacked[:, :, member], 'seq', 0, 0, tiled=True)  15.7 us
    all_to_all x2, starting transfers between devices, shards(): returned.append(lax.all_to_all(attended, 'seq', 0, 0, tiled=True))  14.8 us
    all_to_all x2, waiting for transfers between devices, shards(): returned.append(lax.all_to_all(attended, 'seq', 0, 0, tiled=True))  14.3 us
    unnamed x38, local copies, waits for them, and re-layouts  12.5 us
    dot_general x1, matrix products, shards(): jnp.dot(flat_attended, lax.all_gather(proj_weight, ('cfg', 'seq'), axis=0...  12.2 us
    transpose x1, other arithmetic, shards(): stacked.reshape(3, img_rows, groups, held, HSIZE).transpose(2, 0, 3, 1, 4)  9.26 us
  transfers between devices with their start and end apart: 7, of which 3 were waited for; matrix products, arithmetic and copies ran while one was open for 18% of the time, Pallas kernels for 30%

profile of v2, /device:TPU:6, one launch (start us, length us, event | category | flops | bytes accessed | tf_op | source)
XLA Modules:
  0.0 321.5 jit_solution(18316982191483581247)
XLA Ops:
  9.2 1.1 stack.26
  11.5 8.3 %all-to-all-start.1 = ((bf16[32,2,16,128]{3,2,1,0:T(8,128)(2,1)}), bf16[32,2,16,128]{3,2,1,0:T(8,128)(2,1)S(1)}, u32[]{:S(2)}, u32[]{:S(2)}) async-start(bf16[32,2,16,128]{3,2,1,0:T(8,128)(2,1)} %get-tuple-element.36), calls=%async_computation.1 | async-start | bytes 524288 | tf_op jit(solution)/shard_map/all_to_all | solution.py:191
  19.8 3.5 %copy.27 = f32[1,128,4,2048]{1,3,2,0:T(8,128)} copy(bf16[1,128,4,2048]{3,2,1,0:T(4,128)(2,1)S(1)} %copy-done.8) | data formatting | bytes 6291456 | tf_op jit(solution)/shard_map/convert_element_type | solution.py:178
  23.3 4.9 %copy.24 = f32[1,128,4,2048]{1,3,2,0:T(8,128)} copy(bf16[1,128,4,2048]{3,2,1,0:T(4,128)(2,1)} %param.19) | data formatting | bytes 6291456 | tf_op jit(solution)/shard_map/convert_element_type | solution.py:175
  28.6 6.1 %subtract_convert_fusion.1 = (bf16[128,64,64]{0,2,1:T(8,128)(2,1)}, bf16[128,64,64]{0,2,1:T(8,128)(2,1)}, bf16[128,64,64]{0,2,1:T(8,128)(2,1)S(1)}, bf16[128,64,64]{0,2,1:T(8,128)(2,1)S(1)}) fusion(f32[128,64,128]{0,2,1:T(8,128)} %bitcast.54, f32[128,64]{0,1:T(8,128)S(1)} %get-tuple-element.41, f32[128,64]{0,1:T(8,128)S(1)} %get-tuple-element.40, ...), kind=kLoop, calls=%fused_computation.12 | loop fusion | flops 8388608 | bytes 12648448 | tf_op jit(solution)/shard_map/convert.10
  34.7 2.7 copy.25
  37.4 2.8 copy.26
  40.2 1.8 copy.28
  42.0 1.8 copy.29
  43.8 3.4 %copy.30 = bf16[1,128,4,2048]{1,3,2,0:T(8,128)(2,1)S(1)} copy(bf16[1,128,4,2048]{3,2,1,0:T(4,128)(2,1)} %param.21) | data formatting | bytes 4194304 | tf_op args[4]
  47.2 2.9 copy.31
  50.1 9.3 %maximum_bitcast_fusion = bf16[32,3,2,128,128]{4,3,1,0,2:T(8,128)(2,1)} fusion(bf16[1,128,32,2,128]{4,1,0,2,3:T(8,128)(2,1)} %copy.31, bf16[1,128,32,2,64]{4,1,0,2,3:T(8,128)(2,1)} %copy.29, bf16[1,128,32,2,64]{4,1,0,2,3:T(8,128)(2,1)} %copy.28, bf16[1,128,32,2,64]{4,1,0,2,3:T(8,128)(2,1)} %copy.26, bf16[1,128,32,2,64]{4,1,0,2,3:T(8,128)(2,1)} %copy.25), kind=kLoop, calls=%fused_computation.2 | loop fusion | flops 31457280 | bytes 12582912 | tf_op jit(solution)/shard_map/transpose | solution.py:182
  59.4 7.4 %all-to-all-start.4 = ((bf16[32,2,16,128]{3,2,1,0:T(8,128)(2,1)}), bf16[32,2,16,128]{3,2,1,0:T(8,128)(2,1)S(1)}, u32[]{:S(2)}, u32[]{:S(2)}) async-start(bf16[32,2,16,128]{3,2,1,0:T(8,128)(2,1)} %get-tuple-element.37), calls=%async_computation.4 | async-start | bytes 524288 | tf_op jit(solution)/shard_map/all_to_all | solution.py:191
  66.8 8.3 %slice_bitcast_fusion.1 = (bf16[32,3,128,128]{3,2,1,0:T(8,128)(2,1)}, bf16[32,3,128,128]{3,2,1,0:T(8,128)(2,1)}) fusion(bf16[32,3,2,128,128]{4,3,1,0,2:T(8,128)(2,1)} %maximum_bitcast_fusion), kind=kLoop, calls=%fused_computation.7 | loop fusion | bytes 12582912 | tf_op jit(solution)/shard_map/squeeze | solution.py:190
  75.2 2.2 all-to-all-done.4.kt_ref.vt_ref
  77.4 56.9 %all_to_all.30.q_ref.k_ref.v_ref = bf16[32,3,128,128]{3,2,1,0:T(8,128)(2,1)} all-to-all(bf16[32,3,128,128]{3,2,1,0:T(8,128)(2,1)} %get-tuple-element.28), channel_id=1, replica_groups=mesh['cfg'=2,'seq'=32,'req'=2] {'seq'}, dimensions={0} | all-to-all | bytes 6291456 | tf_op jit(solution)/shard_map/all_to_all | solution.py:190
  134.3 6.0 %all-to-all-start.3 = ((bf16[32,3,128,128]{3,2,1,0:T(8,128)(2,1)}), bf16[32,3,128,128]{3,2,1,0:T(8,128)(2,1)S(1)}, u32[]{:S(2)}, u32[]{:S(2)}) async-start(bf16[32,3,128,128]{3,2,1,0:T(8,128)(2,1)} %get-tuple-element.29), calls=%async_computation.3 | async-start | bytes 6291456 | tf_op jit(solution)/shard_map/all_to_all | solution.py:190
  141.6 1.9 copy-done.1
  144.5 48.5 %shard_map.176 = bf16[32,128,128]{2,1,0:T(8,128)(2,1)S(1)} custom-call(s32[1]{0:T(128)S(6)} %select_n.47.len_ref, bf16[32,3,128,128]{3,2,1,0:T(8,128)(2,1)S(1)} %copy-done.1, bf16[32,3,128,128]{3,2,1,0:T(8,128)(2,1)S(1)} %copy-done.1, bf16[32,3,128,128]{3,2,1,0:T(8,128)(2,1)S(1)} %copy-done.1, bf16[32,2,16,128]{3,2,1,0:T(8,128)(2,1)S(1)} %copy-done.5, ...), custom_call_target="tpu_custom_call" | custom-call | flops 9663676416 | bytes 4456448 | tf_op jit(solution)/shard_map/pallas_call | solution.py:126
  194.0 7.5 %all-to-all-start.2 = ((bf16[32,128,128]{2,1,0:T(8,128)(2,1)}), bf16[32,128,128]{2,1,0:T(8,128)(2,1)}, u32[]{:S(2)}, u32[]{:S(2)}) async-start(bf16[32,128,128]{2,1,0:T(8,128)(2,1)} %copy-done.3), calls=%async_computation.2 | async-start | bytes 2097152 | tf_op jit(solution)/shard_map/all_to_all | solution.py:195
  203.2 48.5 %shard_map.177 = bf16[32,128,128]{2,1,0:T(8,128)(2,1)S(1)} custom-call(s32[1]{0:T(128)S(6)} %select_n.48.len_ref, bf16[32,3,128,128]{3,2,1,0:T(8,128)(2,1)S(1)} %all-to-all-done.3.q_ref.k_ref.v_ref, bf16[32,3,128,128]{3,2,1,0:T(8,128)(2,1)S(1)} %all-to-all-done.3.q_ref.k_ref.v_ref, bf16[32,3,128,128]{3,2,1,0:T(8,128)(2,1)S(1)} %all-to-all-done.3.q_ref.k_ref.v_ref, ...), custom_call_target="tpu_custom_call" | custom-call | flops 9663676416 | bytes 4456448 | tf_op jit(solution)/shard_map/pallas_call | solution.py:126
  252.7 7.3 %all-to-all-start.5 = ((bf16[32,128,128]{2,1,0:T(8,128)(2,1)}), bf16[32,128,128]{2,1,0:T(8,128)(2,1)S(1)}, u32[]{:S(2)}, u32[]{:S(2)}) async-start(bf16[32,128,128]{2,1,0:T(8,128)(2,1)} %copy-done.2), calls=%async_computation.5 | async-start | bytes 2097152 | tf_op jit(solution)/shard_map/all_to_all | solution.py:195
  260.0 1.7 copy.39
  262.5 14.3 %all-to-all-done.5 = bf16[32,128,128]{2,1,0:T(8,128)(2,1)S(1)} async-done(((bf16[32,128,128]{2,1,0:T(8,128)(2,1)}), bf16[32,128,128]{2,1,0:T(8,128)(2,1)S(1)}, u32[]{:S(2)}, u32[]{:S(2)}) %all-to-all-start.5) | async-done | bytes 1048608 | tf_op jit(solution)/shard_map/all_to_all | solution.py:195
  276.8 1.4 pad_maximum_fusion
  278.4 3.0 copy.35
  281.3 12.2 %fusion.6 = (f32[128,4]{0,1:T(4,128)S(1)}, f32[128,4,3072]{2,0,1:T(8,128)S(1)}) fusion(bf16[128,4,2048]{0,2,1:T(8,128)(2,1)} %bitcast.62, bf16[2048,3072]{1,0:T(8,128)(2,1)} %all-gather.2.cloned.1.call-done, f32[4,3072]{1,0:T(4,128)S(1)} %bitcast.66, bf16[1,128,4,3072]{3,2,1,0:T(4,128)(2,1)} %param.18), kind=kOutput, calls=%fused_computation.39 | convolution fusion | flops 6448741888 | bytes 24168448 | tf_op jit(solution)/shard_map/dot_general | solution.py:198
  294.4 1.7 add_convert_fusion
  296.1 2.4 copy.37
  298.5 2.4 reshape.233
  301.0 3.0 convolution_add_fusion
  304.4 8.4 %collective-permute-done = f32[128,4,64]{2,1,0:T(4,128)S(1)} collective-permute-done((f32[128,4,64]{2,1,0:T(4,128)S(1)}, f32[128,4,64]{2,1,0:T(4,128)S(1)}, u32[]{:S(2)}, u32[]{:S(2)}) %collective-permute-start) | collective-permute-done | bytes 131104 | tf_op jit(solution)/shard_map/ppermute | solution.py:19
  (62 shorter events, 11.9 us)
Async XLA Ops:
  7.2 293.8 %copy-start = (bf16[3072,64]{0,1:T(8,128)(2,1)S(1)}, bf16[3072,64]{0,1:T(8,128)(2,1)}, u32[]{:S(2)}) copy-start(bf16[3072,64]{0,1:T(8,128)(2,1)} %param.32) | copy-start | bytes 1179652
  7.2 12.6 %copy-start.8 = (bf16[1,128,4,2048]{3,2,1,0:T(4,128)(2,1)S(1)}, bf16[1,128,4,2048]{3,2,1,0:T(4,128)(2,1)}, u32[]{:S(2)}) copy-start(bf16[1,128,4,2048]{3,2,1,0:T(4,128)(2,1)} %param.20) | copy-start | bytes 6291460
  7.2 274.1 %all-gather.2.cloned.1.call-start = ((), (), s32[]{:S(2)}) async-start(), calls=%async_computation.6 | async-start | bytes 12779520 | tf_op jit(solution)/shard_map/all_gather | solution.py:200
  11.5 47.9 %all-to-all-start.1 = ((bf16[32,2,16,128]{3,2,1,0:T(8,128)(2,1)}), bf16[32,2,16,128]{3,2,1,0:T(8,128)(2,1)S(1)}, u32[]{:S(2)}, u32[]{:S(2)}) async-start(bf16[32,2,16,128]{3,2,1,0:T(8,128)(2,1)} %get-tuple-element.36), calls=%async_computation.1 | async-start | bytes 524288 | tf_op jit(solution)/shard_map/all_to_all | solution.py:191
  23.3 5.0 %copy-start.13 = (s32[3,128]{1,0:T(4,128)S(1)}, s32[3,128]{1,0:T(4,128)}, u32[]{:S(2)}) copy-start(s32[3,128]{1,0:T(4,128)} %param.25) | copy-start | bytes 4612
  59.4 15.8 %copy-start.4 = (bf16[32,2,16,128]{3,2,1,0:T(8,128)(2,1)}, bf16[32,2,16,128]{3,2,1,0:T(8,128)(2,1)S(1)}, u32[]{:S(2)}) copy-start(bf16[32,2,16,128]{3,2,1,0:T(8,128)(2,1)S(1)} %all-to-all-done.1.kt_ref.vt_ref) | copy-start | bytes 786436
  59.4 18.0 %all-to-all-start.4 = ((bf16[32,2,16,128]{3,2,1,0:T(8,128)(2,1)}), bf16[32,2,16,128]{3,2,1,0:T(8,128)(2,1)S(1)}, u32[]{:S(2)}, u32[]{:S(2)}) async-start(bf16[32,2,16,128]{3,2,1,0:T(8,128)(2,1)} %get-tuple-element.37), calls=%async_computation.4 | async-start | bytes 524288 | tf_op jit(solution)/shard_map/all_to_all | solution.py:191
  77.4 56.9 %copy-start.6 = (bf16[32,2,16,128]{3,2,1,0:T(8,128)(2,1)}, bf16[32,2,16,128]{3,2,1,0:T(8,128)(2,1)S(1)}, u32[]{:S(2)}) copy-start(bf16[32,2,16,128]{3,2,1,0:T(8,128)(2,1)S(1)} %all-to-all-done.4.kt_ref.vt_ref) | copy-start | bytes 786436
  134.3 6.0 %copy-start.11 = (s32[1,4]{1,0:T(1,128)S(1)}, s32[1,4]{1,0:T(1,128)}, u32[]{:S(2)}) copy-start(s32[1,4]{1,0:T(1,128)} %param.24) | copy-start | bytes 52
  134.3 59.7 %all-to-all-start.3 = ((bf16[32,3,128,128]{3,2,1,0:T(8,128)(2,1)}), bf16[32,3,128,128]{3,2,1,0:T(8,128)(2,1)S(1)}, u32[]{:S(2)}, u32[]{:S(2)}) async-start(bf16[32,3,128,128]{3,2,1,0:T(8,128)(2,1)} %get-tuple-element.29), calls=%async_computation.3 | async-start | bytes 6291456 | tf_op jit(solution)/shard_map/all_to_all | solution.py:190
  141.6 1.9 copy-start.1
  143.6 1.0 copy-start.5
  193.1 1.0 copy-start.3
  194.0 58.6 %all-to-all-start.2 = ((bf16[32,128,128]{2,1,0:T(8,128)(2,1)}), bf16[32,128,128]{2,1,0:T(8,128)(2,1)}, u32[]{:S(2)}, u32[]{:S(2)}) async-start(bf16[32,128,128]{2,1,0:T(8,128)(2,1)} %copy-done.3), calls=%async_computation.2 | async-start | bytes 2097152 | tf_op jit(solution)/shard_map/all_to_all | solution.py:195
  202.2 1.0 copy-start.7
  251.7 1.0 copy-start.2
  252.7 24.1 %all-to-all-start.5 = ((bf16[32,128,128]{2,1,0:T(8,128)(2,1)}), bf16[32,128,128]{2,1,0:T(8,128)(2,1)S(1)}, u32[]{:S(2)}, u32[]{:S(2)}) async-start(bf16[32,128,128]{2,1,0:T(8,128)(2,1)} %copy-done.2), calls=%async_computation.5 | async-start | bytes 2097152 | tf_op jit(solution)/shard_map/all_to_all | solution.py:195
  278.3 3.0 copy-start.16
  293.6 0.8 copy-start.10
  298.5 2.5 copy-start.12
  301.0 3.4 %copy-start.14 = (s32[4]{0:T(128)S(1)}, s32[4]{0:T(128)}, u32[]{:S(2)}) copy-start(s32[4]{0:T(128)} %param.26) | copy-start | bytes 52
  301.0 3.4 %copy-start.15 = (s32[4]{0:T(128)S(1)}, s32[4]{0:T(128)}, u32[]{:S(2)}) copy-start(s32[4]{0:T(128)} %param.27) | copy-start | bytes 52
  301.0 11.8 %copy-start.9 = (f32[128,4,32]{2,1,0:T(4,128)S(1)}, f32[128,4,32]{2,1,0:T(4,128)}, u32[]{:S(2)}) copy-start(f32[128,4,32]{2,1,0:T(4,128)} %copy.39) | copy-start | bytes 196612
  304.1 8.7 %collective-permute-start = (f32[128,4,64]{2,1,0:T(4,128)S(1)}, f32[128,4,64]{2,1,0:T(4,128)S(1)}, u32[]{:S(2)}, u32[]{:S(2)}) collective-permute-start(f32[128,4,64]{2,1,0:T(4,128)S(1)} %bitcast.63), channel_id=1, source_target_pairs={{0,64},{64,0},{1,65},{65,1},{2,66},{66,2},{3,67},{67,3},{4,68},{68... | collective-permute-start | bytes 393224 | tf_op jit(solution)/shard_map/ppermute | solution.py:19
Sparse Core Ops, SparseCore 0:
  9.7 174.3 all-gather.1

commit v3 on v2

--- a/solution.py
+++ b/solution.py
@@ -137,6 +137,52 @@
             bytes_accessed=(img * 4 + txt * 2) * HSIZE * 2,
         ),
     )(length, chunk, chunk, chunk, text_chunk, text_chunk)
+
+
+def prep_kernel(cs_ref, q_ref, k_ref, v_ref, kt_ref, vt_ref, o_ref, ot_ref):
+    cosine = cs_ref[0]
+    sine = cs_ref[1]
+    prompts = q_ref.shape[1]
+    heads = q_ref.shape[2] // HSIZE
+    held = o_ref.shape[0]
+    per_prompt = heads // held
+    def one_head(h, carry):
+        cols = pl.ds(pl.multiple_of(h * HSIZE, HSIZE), HSIZE)
+        member = h % held
+        for p in range(prompts):
+            dest = p * per_prompt + h // held
+            for t, ref in enumerate((q_ref, k_ref)):
+                x = ref[:, p, cols].astype(jnp.float32)
+                turned = pltpu.roll(x, HSIZE // 2, 1)
+                o_ref[member, dest, t] = (x * cosine + turned * sine).astype(o_ref.dtype)
+            o_ref[member, dest, 2] = v_ref[:, p, cols]
+            ot_ref[member, dest, 0] = kt_ref[:, p, cols]
+            ot_ref[member, dest, 1] = vt_ref[:, p, cols]
+        return carry
+
+    lax.fori_loop(0, heads, one_head, 0)
+
+
+def prep_send(cs, q, k, v, kt, vt, groups):
+    tokens, prompts, width = q.shape
+    text_tokens = kt.shape[0]
+    held = prompts * (width // HSIZE) // groups
+    vmem = pl.BlockSpec(memory_space=pltpu.VMEM)
+    return pl.pallas_call(
+        prep_kernel,
+        in_specs=[vmem] * 6,
+        out_specs=[vmem, vmem],
+        out_shape=[
+            jax.ShapeDtypeStruct((held, groups, 3, tokens, HSIZE), jnp.bfloat16),
+            jax.ShapeDtypeStruct((held, groups, 2, text_tokens, HSIZE), jnp.bfloat16),
+        ],
+        compiler_params=pltpu.CompilerParams(vmem_limit_bytes=48 * 1024 * 1024),
+        cost_estimate=pl.CostEstimate(
+            flops=tokens * prompts * width * 12,
+            transcendentals=0,
+            bytes_accessed=(tokens * 3 + text_tokens * 2) * prompts * width * 4,
+        ),
+    )(cs, q, k, v, kt, vt)
 
 
 def roster(fraction):
@@ -170,25 +216,21 @@
     members = prompt_count * head_count
     groups = lax.axis_size("seq")
     held = members // groups
-    angle = rope_angles(img_ids)[:, None, :]
-    rot_query = rotate(
-        query_img[0].reshape(img_rows, members, HSIZE).astype(jnp.float32), angle
-    ).astype(jnp.bfloat16)
-    rot_key = rotate(
-        key_img[0].reshape(img_rows, members, HSIZE).astype(jnp.float32), angle
-    ).astype(jnp.bfloat16)
-    vals = value_img[0].reshape(img_rows, members, HSIZE)
-    stacked = jnp.stack([rot_query, rot_key, vals])
-    stacked = stacked.reshape(3, img_rows, groups, held, HSIZE).transpose(2, 0, 3, 1, 4)
-    text_stacked = jnp.stack(
-        [key_txt[0].reshape(text_rows, members, HSIZE), value_txt[0].reshape(text_rows, members, HSIZE)]
-    )
-    text_stacked = text_stacked.reshape(2, text_rows, groups, held, HSIZE).transpose(2, 0, 3, 1, 4)
+    angle = rope_angles(img_ids)
+    cosine = jnp.cos(angle)
+    sine = jnp.sin(angle)
+    cs = jnp.stack([
+        jnp.concatenate([cosine, cosine], axis=1),
+        jnp.concatenate([-sine, sine], axis=1),
+    ])
+    stacked, text_stacked = prep_send(
+        cs, query_img[0], key_img[0], value_img[0], key_txt[0], value_txt[0], groups
+    )
     first_member = lax.axis_index("seq") * held
     returned = []
     for member in range(held):
-        got = lax.all_to_all(stacked[:, :, member], "seq", 0, 0, tiled=True)
-        got_text = lax.all_to_all(text_stacked[:, :, member], "seq", 0, 0, tiled=True)
+        got = lax.all_to_all(stacked[member], "seq", 0, 0, tiled=True)
+        got_text = lax.all_to_all(text_stacked[member], "seq", 0, 0, tiled=True)
         prompt_of = (first_member + member) // head_count
         length = jnp.take(text_len[0], prompt_of)[None]
         attended = attend_member(got, got_text, length)

time: 323 us -> 315 us (0.975)
  local copies, waits for them, and re-layouts: 53.4 us -> 31.8 us
  Pallas kernels: 97.1 us -> 117 us
  blocking collectives: 56.9 us -> 75.9 us
  other arithmetic: 20.8 us -> 6.47 us
  starting transfers between devices: 36.9 us -> 26.1 us
    pallas_call x0 -> x1, Pallas kernels: none -> 19.9 us  [prep_send(): pl.pallas_call(prep_kernel, in_specs=[vmem] * 6, out_specs=[vmem, vmem],...]
    all_to_all x1 -> x2, blocking collectives: 56.9 us -> 75.9 us  [the longest x1 56.8 us: shards(): got = lax.all_to_all(stacked[member], 'seq', 0, 0, tiled=True)]
    all_to_all x3 -> x2, starting transfers between devices: 21.7 us -> 10.9 us  [the longest x1 6.63 us: shards(): got = lax.all_to_all(stacked[member], 'seq', 0, 0, tiled=True)]
    transpose x2 -> x0, other arithmetic: 9.33 us -> none  [the longest x1 9.26 us: shards(): stacked.reshape(3, img_rows, groups, held, HSIZE).transpose(2, 0, 3, 1, 4)]
    concatenate x4 -> x0, local copies, waits for them, and re-layouts: 9.09 us -> none  [rotate(): jnp.concatenate([first * cosine - second * sine, first * sine + second *...]
    convert_element_type x2 -> x0, local copies, waits for them, and re-layouts: 8.43 us -> none  [the longest x1 4.95 us: shards(): query_img[0].reshape(img_rows, members, HSIZE).astype(jnp.float32)]
    another operation x1 -> x2, other arithmetic: 6.1 us -> 0.11 us  [shards(): jnp.stack([jnp.concatenate([cosine, cosine], axis=1), jnp.concatenate([-s...]
    another operation x5 -> x0, local copies, waits for them, and re-layouts: 5.49 us -> none  [the longest x1 2.91 us: shards(): stacked = jnp.stack([rot_query, rot_key, vals])]
  transfers between devices with their start and end apart: 7 -> 6, of which waited for: 3 -> 3; matrix products, arithmetic and copies ran while one was open for 18% -> 6% of each run, Pallas kernels for 30% -> 37%
where the time goes in v3:
time: 315 us; the launch traced here: 314 us
  Pallas kernels  117 us (37%)
  blocking collectives  75.9 us (24%)
  local copies, waits for them, and re-layouts  31.8 us (10%)
  starting transfers between devices  26.1 us (8%)
  waiting for transfers between devices  25.6 us (8%)
  between operations  15.7 us (5%)
  matrix products  15.3 us (5%)
  other arithmetic  6.47 us (2%)
    pallas_call x2, Pallas kernels, attend_member(): pl.pallas_call(attend_kernel, grid_spec=grid_spec, out_shape=jax.ShapeDty...  97.1 us
    all_to_all x1, blocking collectives, shards(): got = lax.all_to_all(stacked[member], 'seq', 0, 0, tiled=True)  56.8 us
    pallas_call x1, Pallas kernels, prep_send(): pl.pallas_call(prep_kernel, in_specs=[vmem] * 6, out_specs=[vmem, vmem],...  19.9 us
    all_to_all x1, blocking collectives, shards(): got_text = lax.all_to_all(text_stacked[member], 'seq', 0, 0, tiled=True)  19.1 us
    all_to_all x2, starting transfers between devices, shards(): returned.append(lax.all_to_all(attended, 'seq', 0, 0, tiled=True))  15 us
    all_to_all x2, waiting for transfers between devices, shards(): returned.append(lax.all_to_all(attended, 'seq', 0, 0, tiled=True))  14.1 us
    unnamed x39, local copies, waits for them, and re-layouts  14.1 us
    dot_general x1, matrix products, shards(): jnp.dot(flat_attended, lax.all_gather(proj_weight, ('cfg', 'seq'), axis=0...  12.2 us
  transfers between devices with their start and end apart: 6, of which 3 were waited for; matrix products, arithmetic and copies ran while one was open for 6% of the time, Pallas kernels for 37%

profile of v3, /device:TPU:6, one launch (start us, length us, event | category | flops | bytes accessed | tf_op | source)
XLA Modules:
  0.0 313.7 jit_solution(17689167666792039708)
XLA Ops:
  7.9 0.8 convert_bitcast_fusion.2
  9.4 1.6 copy-done.2
  11.0 1.6 copy-done.3
  12.6 0.9 copy-done.9
  13.5 0.9 copy-done.10
  14.5 19.9 %shard_map.176 = (bf16[2,32,3,128,128]{4,3,2,1,0:T(8,128)(2,1)}, bf16[2,32,2,16,128]{4,3,2,1,0:T(8,128)(2,1)S(1)}) custom-call(f32[2,128,128]{2,1,0:T(8,128)S(1)} %pad_maximum_fusion.1.cs_ref, bf16[128,4,2048]{2,1,0:T(4,128)(2,1)S(1)} %bitcast.51, bf16[128,4,2048]{2,1,0:T(4,128)(2,1)S(1)} %bitcast.52, bf16[128,4,2048]{2,1,0:T(4,128)(2,1)} %bitcast.57, ...), custom_call_target="tpu_custom_call" | custom-call | flops 12582912 | bytes 13631488 | tf_op jit(solution)/shard_map/pallas_call | solution.py:171
  35.2 19.1 %all_to_all.30.kt_ref.vt_ref = bf16[32,2,16,128]{3,2,1,0:T(8,128)(2,1)} all-to-all(bf16[32,2,16,128]{3,2,1,0:T(8,128)(2,1)S(1)} %get-tuple-element.38), channel_id=1, replica_groups=mesh['cfg'=2,'seq'=32,'req'=2] {'seq'}, dimensions={0} | all-to-all | bytes 524288 | tf_op jit(solution)/shard_map/all_to_all | solution.py:233
  54.2 4.3 %all-to-all-start.4 = ((bf16[32,2,16,128]{3,2,1,0:T(8,128)(2,1)}), bf16[32,2,16,128]{3,2,1,0:T(8,128)(2,1)S(1)}, u32[]{:S(2)}, u32[]{:S(2)}) async-start(bf16[32,2,16,128]{3,2,1,0:T(8,128)(2,1)} %get-tuple-element.39), calls=%async_computation.4 | async-start | bytes 524288 | tf_op jit(solution)/shard_map/all_to_all | solution.py:233
  58.6 8.3 %slice_bitcast_fusion.1 = (bf16[32,3,128,128]{3,2,1,0:T(8,128)(2,1)}, bf16[32,3,128,128]{3,2,1,0:T(8,128)(2,1)}) fusion(bf16[2,32,3,128,128]{4,3,2,1,0:T(8,128)(2,1)} %get-tuple-element.4), kind=kLoop, calls=%fused_computation.6 | loop fusion | bytes 12582912 | tf_op jit(solution)/shard_map/squeeze | solution.py:232
  66.9 2.3 all-to-all-done.4.kt_ref.vt_ref
  69.1 56.8 %all_to_all.31.q_ref.k_ref.v_ref = bf16[32,3,128,128]{3,2,1,0:T(8,128)(2,1)} all-to-all(bf16[32,3,128,128]{3,2,1,0:T(8,128)(2,1)} %get-tuple-element.34), channel_id=1, replica_groups=mesh['cfg'=2,'seq'=32,'req'=2] {'seq'}, dimensions={0} | all-to-all | bytes 6291456 | tf_op jit(solution)/shard_map/all_to_all | solution.py:232
  125.9 6.6 %all-to-all-start.3 = ((bf16[32,3,128,128]{3,2,1,0:T(8,128)(2,1)}), bf16[32,3,128,128]{3,2,1,0:T(8,128)(2,1)S(1)}, u32[]{:S(2)}, u32[]{:S(2)}) async-start(bf16[32,3,128,128]{3,2,1,0:T(8,128)(2,1)} %get-tuple-element.35), calls=%async_computation.3 | async-start | bytes 6291456 | tf_op jit(solution)/shard_map/all_to_all | solution.py:232
  133.9 1.9 copy-done.1
  135.8 1.0 copy-done.8
  136.7 48.5 %shard_map.177 = bf16[32,128,128]{2,1,0:T(8,128)(2,1)S(1)} custom-call(s32[1]{0:T(128)S(6)} %select_n.47.len_ref, bf16[32,3,128,128]{3,2,1,0:T(8,128)(2,1)S(1)} %copy-done.1, bf16[32,3,128,128]{3,2,1,0:T(8,128)(2,1)S(1)} %copy-done.1, bf16[32,3,128,128]{3,2,1,0:T(8,128)(2,1)S(1)} %copy-done.1, bf16[32,2,16,128]{3,2,1,0:T(8,128)(2,1)S(1)} %copy-done.8, ...), custom_call_target="tpu_custom_call" | custom-call | flops 9663676416 | bytes 4456448 | tf_op jit(solution)/shard_map/pallas_call | solution.py:126
  185.3 1.0 copy-done.5
  186.2 7.5 %all-to-all-start.2 = ((bf16[32,128,128]{2,1,0:T(8,128)(2,1)}), bf16[32,128,128]{2,1,0:T(8,128)(2,1)}, u32[]{:S(2)}, u32[]{:S(2)}) async-start(bf16[32,128,128]{2,1,0:T(8,128)(2,1)} %copy-done.5), calls=%async_computation.2 | async-start | bytes 2097152 | tf_op jit(solution)/shard_map/all_to_all | solution.py:237
  194.4 0.9 copy-done.7
  195.4 48.5 %shard_map.178 = bf16[32,128,128]{2,1,0:T(8,128)(2,1)S(1)} custom-call(s32[1]{0:T(128)S(6)} %select_n.48.len_ref, bf16[32,3,128,128]{3,2,1,0:T(8,128)(2,1)S(1)} %all-to-all-done.3.q_ref.k_ref.v_ref, bf16[32,3,128,128]{3,2,1,0:T(8,128)(2,1)S(1)} %all-to-all-done.3.q_ref.k_ref.v_ref, bf16[32,3,128,128]{3,2,1,0:T(8,128)(2,1)S(1)} %all-to-all-done.3.q_ref.k_ref.v_ref, ...), custom_call_target="tpu_custom_call" | custom-call | flops 9663676416 | bytes 4456448 | tf_op jit(solution)/shard_map/pallas_call | solution.py:126
  243.9 1.0 copy-done.4
  244.9 7.5 %all-to-all-start.5 = ((bf16[32,128,128]{2,1,0:T(8,128)(2,1)}), bf16[32,128,128]{2,1,0:T(8,128)(2,1)S(1)}, u32[]{:S(2)}, u32[]{:S(2)}) async-start(bf16[32,128,128]{2,1,0:T(8,128)(2,1)} %copy-done.4), calls=%async_computation.5 | async-start | bytes 2097152 | tf_op jit(solution)/shard_map/all_to_all | solution.py:237
  252.4 1.7 copy.29
  254.1 0.8 add_bitcast_fusion
  254.9 14.1 %all-to-all-done.5 = bf16[32,128,128]{2,1,0:T(8,128)(2,1)S(1)} async-done(((bf16[32,128,128]{2,1,0:T(8,128)(2,1)}), bf16[32,128,128]{2,1,0:T(8,128)(2,1)S(1)}, u32[]{:S(2)}, u32[]{:S(2)}) %all-to-all-start.5) | async-done | bytes 1048608 | tf_op jit(solution)/shard_map/all_to_all | solution.py:237
  269.0 1.4 pad_maximum_fusion
  270.6 3.0 copy.25
  273.5 12.2 %fusion.8 = (f32[128,4]{0,1:T(4,128)S(1)}, f32[128,4,3072]{2,0,1:T(8,128)S(1)}) fusion(bf16[128,4,2048]{0,2,1:T(8,128)(2,1)} %bitcast.58, bf16[2048,3072]{1,0:T(8,128)(2,1)} %all-gather.2.cloned.1.call-done, f32[4,3072]{1,0:T(4,128)S(1)} %bitcast.62, bf16[1,128,4,3072]{3,2,1,0:T(4,128)(2,1)} %param.18), kind=kOutput, calls=%fused_computation.37 | convolution fusion | flops 6448741888 | bytes 24168448 | tf_op jit(solution)/shard_map/dot_general | solution.py:240
  286.6 1.7 add_convert_fusion
  288.3 2.4 copy.27
  290.7 2.4 reshape.67
  293.2 3.0 convolution_add_fusion
  296.5 8.6 %collective-permute-done = f32[128,4,64]{2,1,0:T(4,128)S(1)} collective-permute-done((f32[128,4,64]{2,1,0:T(4,128)S(1)}, f32[128,4,64]{2,1,0:T(4,128)S(1)}, u32[]{:S(2)}, u32[]{:S(2)}) %collective-permute-start) | collective-permute-done | bytes 131104 | tf_op jit(solution)/shard_map/ppermute | solution.py:19
  (51 shorter events, 5.8 us)
Async XLA Ops:
  7.2 286.0 %copy-start = (bf16[3072,64]{0,1:T(8,128)(2,1)S(1)}, bf16[3072,64]{0,1:T(8,128)(2,1)}, u32[]{:S(2)}) copy-start(bf16[3072,64]{0,1:T(8,128)(2,1)} %param.32) | copy-start | bytes 1179652
  7.2 266.4 %all-gather.2.cloned.1.call-start = ((), (), s32[]{:S(2)}) async-start(), calls=%async_computation.6 | async-start | bytes 12779520 | tf_op jit(solution)/shard_map/all_gather | solution.py:242
  9.4 1.6 copy-start.2
  11.0 1.6 copy-start.3
  12.6 0.9 copy-start.9
  13.5 0.9 copy-start.10
  54.2 14.9 %all-to-all-start.4 = ((bf16[32,2,16,128]{3,2,1,0:T(8,128)(2,1)}), bf16[32,2,16,128]{3,2,1,0:T(8,128)(2,1)S(1)}, u32[]{:S(2)}, u32[]{:S(2)}) async-start(bf16[32,2,16,128]{3,2,1,0:T(8,128)(2,1)} %get-tuple-element.39), calls=%async_computation.4 | async-start | bytes 524288 | tf_op jit(solution)/shard_map/all_to_all | solution.py:233
  69.1 56.8 %copy-start.6 = (bf16[32,2,16,128]{3,2,1,0:T(8,128)(2,1)}, bf16[32,2,16,128]{3,2,1,0:T(8,128)(2,1)S(1)}, u32[]{:S(2)}) copy-start(bf16[32,2,16,128]{3,2,1,0:T(8,128)(2,1)S(1)} %all-to-all-done.4.kt_ref.vt_ref) | copy-start | bytes 786436
  125.9 6.7 %copy-start.13 = (s32[1,4]{1,0:T(1,128)S(1)}, s32[1,4]{1,0:T(1,128)}, u32[]{:S(2)}) copy-start(s32[1,4]{1,0:T(1,128)} %param.24) | copy-start | bytes 52
  125.9 60.3 %all-to-all-start.3 = ((bf16[32,3,128,128]{3,2,1,0:T(8,128)(2,1)}), bf16[32,3,128,128]{3,2,1,0:T(8,128)(2,1)S(1)}, u32[]{:S(2)}, u32[]{:S(2)}) async-start(bf16[32,3,128,128]{3,2,1,0:T(8,128)(2,1)} %get-tuple-element.35), calls=%async_computation.3 | async-start | bytes 6291456 | tf_op jit(solution)/shard_map/all_to_all | solution.py:232
  133.8 1.9 copy-start.1
  135.8 1.0 copy-start.8
  185.3 1.0 copy-start.5
  186.2 58.6 %all-to-all-start.2 = ((bf16[32,128,128]{2,1,0:T(8,128)(2,1)}), bf16[32,128,128]{2,1,0:T(8,128)(2,1)}, u32[]{:S(2)}, u32[]{:S(2)}) async-start(bf16[32,128,128]{2,1,0:T(8,128)(2,1)} %copy-done.5), calls=%async_computation.2 | async-start | bytes 2097152 | tf_op jit(solution)/shard_map/all_to_all | solution.py:237
  194.4 1.0 copy-start.7
  243.9 1.0 copy-start.4
  244.9 24.1 %all-to-all-start.5 = ((bf16[32,128,128]{2,1,0:T(8,128)(2,1)}), bf16[32,128,128]{2,1,0:T(8,128)(2,1)S(1)}, u32[]{:S(2)}, u32[]{:S(2)}) async-start(bf16[32,128,128]{2,1,0:T(8,128)(2,1)} %copy-done.4), calls=%async_computation.5 | async-start | bytes 2097152 | tf_op jit(solution)/shard_map/all_to_all | solution.py:237
  270.6 3.0 copy-start.17
  285.8 0.8 copy-start.12
  290.7 2.5 copy-start.14
  293.2 3.3 %copy-start.15 = (s32[4]{0:T(128)S(1)}, s32[4]{0:T(128)}, u32[]{:S(2)}) copy-start(s32[4]{0:T(128)} %param.26) | copy-start | bytes 52
  293.2 3.3 %copy-start.16 = (s32[4]{0:T(128)S(1)}, s32[4]{0:T(128)}, u32[]{:S(2)}) copy-start(s32[4]{0:T(128)} %param.27) | copy-start | bytes 52
  293.2 11.8 %copy-start.11 = (f32[128,4,32]{2,1,0:T(4,128)S(1)}, f32[128,4,32]{2,1,0:T(4,128)}, u32[]{:S(2)}) copy-start(f32[128,4,32]{2,1,0:T(4,128)} %copy.29) | copy-start | bytes 196612
  296.4 8.7 %collective-permute-start = (f32[128,4,64]{2,1,0:T(4,128)S(1)}, f32[128,4,64]{2,1,0:T(4,128)S(1)}, u32[]{:S(2)}, u32[]{:S(2)}) collective-permute-start(f32[128,4,64]{2,1,0:T(4,128)S(1)} %bitcast.59), channel_id=1, source_target_pairs={{0,64},{64,0},{1,65},{65,1},{2,66},{66,2},{3,67},{67,3},{4,68},{68... | collective-permute-start | bytes 393224 | tf_op jit(solution)/shard_map/ppermute | solution.py:19
Sparse Core Ops, SparseCore 0:
  9.7 177.7 all-gather.1

commit v4 on v3

--- a/solution.py
+++ b/solution.py
@@ -99,21 +99,21 @@
     o_ref[...] = (acc_scr[...] / denom).astype(o_ref.dtype).reshape(o_ref.shape)
 
 
-def attend_member(chunk, text_chunk, length):
-    sources, tokens = chunk.shape[0], chunk.shape[2]
-    text_tokens = text_chunk.shape[2]
+def attend_member(chunk, tokens, text_tokens, length):
+    sources = chunk.shape[0]
     img = sources * tokens
     txt = sources * text_tokens
     per_block = QBLOCK // tokens
+    text_at = 3 * tokens // text_tokens
     grid_spec = pltpu.PrefetchScalarGridSpec(
         num_scalar_prefetch=1,
         grid=(img // QBLOCK,),
         in_specs=[
-            pl.BlockSpec((per_block, None, tokens, HSIZE), lambda i, lens: (i, 0, 0, 0)),
-            pl.BlockSpec((sources, None, tokens, HSIZE), lambda i, lens: (0, 1, 0, 0)),
-            pl.BlockSpec((sources, None, tokens, HSIZE), lambda i, lens: (0, 2, 0, 0)),
-            pl.BlockSpec((sources, None, text_tokens, HSIZE), lambda i, lens: (0, 0, 0, 0)),
-            pl.BlockSpec((sources, None, text_tokens, HSIZE), lambda i, lens: (0, 1, 0, 0)),
+            pl.BlockSpec((per_block, tokens, HSIZE), lambda i, lens: (i, 0, 0)),
+            pl.BlockSpec((sources, tokens, HSIZE), lambda i, lens: (0, 1, 0)),
+            pl.BlockSpec((sources, tokens, HSIZE), lambda i, lens: (0, 2, 0)),
+            pl.BlockSpec((sources, text_tokens, HSIZE), lambda i, lens: (0, text_at, 0)),
+            pl.BlockSpec((sources, text_tokens, HSIZE), lambda i, lens: (0, text_at + 1, 0)),
         ],
         out_specs=pl.BlockSpec((per_block, tokens, HSIZE), lambda i, lens: (i, 0, 0)),
         scratch_shapes=[
@@ -136,46 +136,49 @@
             transcendentals=img * (img + txt),
             bytes_accessed=(img * 4 + txt * 2) * HSIZE * 2,
         ),
-    )(length, chunk, chunk, chunk, text_chunk, text_chunk)
-
-
-def prep_kernel(cs_ref, q_ref, k_ref, v_ref, kt_ref, vt_ref, o_ref, ot_ref):
+    )(length, chunk, chunk, chunk, chunk, chunk)
+
+
+def prep_kernel(cs_ref, q_ref, k_ref, v_ref, kt_ref, vt_ref, *out_refs):
     cosine = cs_ref[0]
     sine = cs_ref[1]
-    prompts = q_ref.shape[1]
+    tokens, prompts = q_ref.shape[0], q_ref.shape[1]
+    text_tokens = kt_ref.shape[0]
     heads = q_ref.shape[2] // HSIZE
-    held = o_ref.shape[0]
+    held = len(out_refs)
     per_prompt = heads // held
-    def one_head(h, carry):
-        cols = pl.ds(pl.multiple_of(h * HSIZE, HSIZE), HSIZE)
-        member = h % held
-        for p in range(prompts):
-            dest = p * per_prompt + h // held
-            for t, ref in enumerate((q_ref, k_ref)):
-                x = ref[:, p, cols].astype(jnp.float32)
-                turned = pltpu.roll(x, HSIZE // 2, 1)
-                o_ref[member, dest, t] = (x * cosine + turned * sine).astype(o_ref.dtype)
-            o_ref[member, dest, 2] = v_ref[:, p, cols]
-            ot_ref[member, dest, 0] = kt_ref[:, p, cols]
-            ot_ref[member, dest, 1] = vt_ref[:, p, cols]
+    img_part = 3 * tokens
+
+    def one_pair(hh, carry):
+        for member in range(held):
+            o_ref = out_refs[member]
+            cols = pl.ds(pl.multiple_of((hh * held + member) * HSIZE, HSIZE), HSIZE)
+            for p in range(prompts):
+                dest = p * per_prompt + hh
+                for t, ref in enumerate((q_ref, k_ref)):
+                    x = ref[:, p, cols].astype(jnp.float32)
+                    turned = pltpu.roll(x, HSIZE // 2, 1)
+                    o_ref[dest, t * tokens:(t + 1) * tokens] = (
+                        x * cosine + turned * sine).astype(o_ref.dtype)
+                o_ref[dest, 2 * tokens:img_part] = v_ref[:, p, cols]
+                o_ref[dest, img_part:img_part + text_tokens] = kt_ref[:, p, cols]
+                o_ref[dest, img_part + text_tokens:img_part + 2 * text_tokens] = vt_ref[:, p, cols]
         return carry
 
-    lax.fori_loop(0, heads, one_head, 0)
+    lax.fori_loop(0, per_prompt, one_pair, 0)
 
 
 def prep_send(cs, q, k, v, kt, vt, groups):
     tokens, prompts, width = q.shape
     text_tokens = kt.shape[0]
     held = prompts * (width // HSIZE) // groups
+    rows = 3 * tokens + 2 * text_tokens
     vmem = pl.BlockSpec(memory_space=pltpu.VMEM)
     return pl.pallas_call(
         prep_kernel,
         in_specs=[vmem] * 6,
-        out_specs=[vmem, vmem],
-        out_shape=[
-            jax.ShapeDtypeStruct((held, groups, 3, tokens, HSIZE), jnp.bfloat16),
-            jax.ShapeDtypeStruct((held, groups, 2, text_tokens, HSIZE), jnp.bfloat16),
-        ],
+        out_specs=[vmem] * held,
+        out_shape=[jax.ShapeDtypeStruct((groups, rows, HSIZE), jnp.bfloat16)] * held,
         compiler_params=pltpu.CompilerParams(vmem_limit_bytes=48 * 1024 * 1024),
         cost_estimate=pl.CostEstimate(
             flops=tokens * prompts * width * 12,
@@ -223,17 +226,16 @@
         jnp.concatenate([cosine, cosine], axis=1),
         jnp.concatenate([-sine, sine], axis=1),
     ])
-    stacked, text_stacked = prep_send(
+    sends = prep_send(
         cs, query_img[0], key_img[0], value_img[0], key_txt[0], value_txt[0], groups
     )
     first_member = lax.axis_index("seq") * held
     returned = []
     for member in range(held):
-        got = lax.all_to_all(stacked[member], "seq", 0, 0, tiled=True)
-        got_text = lax.all_to_all(text_stacked[member], "seq", 0, 0, tiled=True)
+        got = lax.all_to_all(sends[member], "seq", 0, 0, tiled=True)
         prompt_of = (first_member + member) // head_count
         length = jnp.take(text_len[0], prompt_of)[None]
-        attended = attend_member(got, got_text, length)
+        attended = attend_member(got, img_rows, text_rows, length)
         returned.append(lax.all_to_all(attended, "seq", 0, 0, tiled=True))
     returned = jnp.stack(returned, axis=1).reshape(members, img_rows, HSIZE).transpose(1, 0, 2)
     flat_attended = returned.reshape(img_rows * prompt_count, feature_width)

time: 315 us -> 285 us (0.905)
  local copies, waits for them, and re-layouts: 31.8 us -> 18.2 us
  blocking collectives: 75.9 us -> 63.5 us
  starting transfers between devices: 26.1 us -> 19.8 us
    all_to_all x2 -> x1, blocking collectives: 75.9 us -> 63.5 us  [shards(): got = lax.all_to_all(sends[member], 'seq', 0, 0, tiled=True)]
    squeeze x2 -> x0, local copies, waits for them, and re-layouts: 9.05 us -> none  [the longest x1 8.29 us: shards(): got = lax.all_to_all(stacked[member], 'seq', 0, 0, tiled=True)]
    all_to_all x2 -> x1, starting transfers between devices: 10.9 us -> 5.94 us  [shards(): got = lax.all_to_all(sends[member], 'seq', 0, 0, tiled=True)]
    unnamed x39 -> x33, local copies, waits for them, and re-layouts: 14.1 us -> 9.47 us
    all_to_all x2, starting transfers between devices: 15 us -> 11.5 us  [shards(): returned.append(lax.all_to_all(attended, 'seq', 0, 0, tiled=True))]
  transfers between devices with their start and end apart: 6 -> 5, of which waited for: 3 -> 3; matrix products, arithmetic and copies ran while one was open for 6% -> 2% of each run, Pallas kernels for 37% -> 42%
where the time goes in v4:
time: 285 us; the launch traced here: 283 us
  Pallas kernels  120 us (42%)
  blocking collectives  63.5 us (22%)
  waiting for transfers between devices  26.7 us (9%)
  starting transfers between devices  19.8 us (7%)
  local copies, waits for them, and re-layouts  18.2 us (6%)
  between operations  15.6 us (5%)
  matrix products  15.3 us (5%)
  other arithmetic  4.45 us (2%)
    pallas_call x2, Pallas kernels, attend_member(): pl.pallas_call(attend_kernel, grid_spec=grid_spec, out_shape=jax.ShapeDty...  100 us
    all_to_all x1, blocking collectives, shards(): got = lax.all_to_all(sends[member], 'seq', 0, 0, tiled=True)  63.5 us
    pallas_call x1, Pallas kernels, prep_send(): pl.pallas_call(prep_kernel, in_specs=[vmem] * 6, out_specs=[vmem] * held,...  19.7 us
    all_to_all x2, waiting for transfers between devices, shards(): returned.append(lax.all_to_all(attended, 'seq', 0, 0, tiled=True))  15.7 us
    dot_general x1, matrix products, shards(): jnp.dot(flat_attended, lax.all_gather(proj_weight, ('cfg', 'seq'), axis=0...  12.3 us
    all_to_all x2, starting transfers between devices, shards(): returned.append(lax.all_to_all(attended, 'seq', 0, 0, tiled=True))  11.5 us
    unnamed x33, local copies, waits for them, and re-layouts  9.47 us
    ppermute x1, waiting for transfers between devices, partner_2(): return lax.ppermute(value, axis, pairs)  6.85 us
  transfers between devices with their start and end apart: 5, of which 3 were waited for; matrix products, arithmetic and copies ran while one was open for 2% of the time, Pallas kernels for 42%

profile of v4, /device:TPU:6, one launch (start us, length us, event | category | flops | bytes accessed | tf_op | source)
XLA Modules:
  0.0 283.3 jit_solution(7306761512829096035)
XLA Ops:
  7.2 0.7 all-gather.2.cloned.1.call-update
  7.9 0.8 convert_bitcast_fusion.2
  8.9 0.3 fusion.6
  9.4 1.6 copy-done.2
  11.0 1.6 copy-done.3
  12.6 0.9 copy-done.4
  13.5 0.9 copy-done.5
  14.5 19.7 %shard_map.176 = (bf16[32,416,128]{2,1,0:T(8,128)(2,1)}, bf16[32,416,128]{2,1,0:T(8,128)(2,1)}) custom-call(f32[2,128,128]{2,1,0:T(8,128)S(1)} %pad_maximum_fusion.1.cs_ref, bf16[128,4,2048]{2,1,0:T(4,128)(2,1)S(1)} %bitcast.43, bf16[128,4,2048]{2,1,0:T(4,128)(2,1)S(1)} %bitcast.44, bf16[128,4,2048]{2,1,0:T(4,128)(2,1)} %bitcast.50, ...), custom_call_target="tpu_custom_call" | custom-call | flops 12582912 | bytes 13631488 | tf_op jit(solution)/shard_map/pallas_call | solution.py:177
  34.2 63.5 %all_to_all.20.q_ref.k_ref.v_ref.kt_ref.vt_ref = bf16[32,416,128]{2,1,0:T(8,128)(2,1)} all-to-all(bf16[32,416,128]{2,1,0:T(8,128)(2,1)} %get-tuple-element.4), channel_id=1, replica_groups=mesh['cfg'=2,'seq'=32,'req'=2] {'seq'}, dimensions={0} | all-to-all | bytes 6815744 | tf_op jit(solution)/shard_map/all_to_all | solution.py:235
  97.7 5.9 %all-to-all-start.2 = ((bf16[32,416,128]{2,1,0:T(8,128)(2,1)}), bf16[32,416,128]{2,1,0:T(8,128)(2,1)}, u32[]{:S(2)}, u32[]{:S(2)}) async-start(bf16[32,416,128]{2,1,0:T(8,128)(2,1)} %get-tuple-element.5), calls=%async_computation.2 | async-start | bytes 6815744 | tf_op jit(solution)/shard_map/all_to_all | solution.py:235
  103.7 0.6 constant_dynamic-slice_fusion.1
  104.9 2.0 copy-done.1
  106.9 49.2 %shard_map.177 = bf16[32,128,128]{2,1,0:T(8,128)(2,1)} custom-call(s32[1]{0:T(128)S(6)} %select_n.47.len_ref, bf16[32,416,128]{2,1,0:T(8,128)(2,1)S(1)} %copy-done.1, bf16[32,416,128]{2,1,0:T(8,128)(2,1)S(1)} %copy-done.1, bf16[32,416,128]{2,1,0:T(8,128)(2,1)S(1)} %copy-done.1, bf16[32,416,128]{2,1,0:T(8,128)(2,1)S(1)} %copy-done.1, ...), custom_call_target="tpu_custom_call" | custom-call | flops 9663676416 | bytes 4456448 | tf_op jit(solution)/shard_map/pallas_call | solution.py:126
  156.2 3.4 %all-to-all-done.2.q_ref.k_ref.v_ref.kt_ref.vt_ref = bf16[32,416,128]{2,1,0:T(8,128)(2,1)} async-done(((bf16[32,416,128]{2,1,0:T(8,128)(2,1)}), bf16[32,416,128]{2,1,0:T(8,128)(2,1)}, u32[]{:S(2)}, u32[]{:S(2)}) %all-to-all-start.2) | async-done | bytes 3407904 | tf_op jit(solution)/shard_map/all_to_all | solution.py:235
  159.6 3.9 %all-to-all-start.1 = ((bf16[32,128,128]{2,1,0:T(8,128)(2,1)}), bf16[32,128,128]{2,1,0:T(8,128)(2,1)S(1)}, u32[]{:S(2)}, u32[]{:S(2)}) async-start(bf16[32,128,128]{2,1,0:T(8,128)(2,1)} %shard_map.177), calls=%async_computation.1 | async-start | bytes 2097152 | tf_op jit(solution)/shard_map/all_to_all | solution.py:239
  164.2 50.8 %shard_map.178 = bf16[32,128,128]{2,1,0:T(8,128)(2,1)} custom-call(s32[1]{0:T(128)S(6)} %select_n.48.len_ref, bf16[32,416,128]{2,1,0:T(8,128)(2,1)} %all-to-all-done.2.q_ref.k_ref.v_ref.kt_ref.vt_ref, bf16[32,416,128]{2,1,0:T(8,128)(2,1)} %all-to-all-done.2.q_ref.k_ref.v_ref.kt_ref.vt_ref, ...), custom_call_target="tpu_custom_call" | custom-call | flops 9663676416 | bytes 4456448 | tf_op jit(solution)/shard_map/pallas_call | solution.py:126
  215.0 7.6 %all-to-all-start.3 = ((bf16[32,128,128]{2,1,0:T(8,128)(2,1)}), bf16[32,128,128]{2,1,0:T(8,128)(2,1)S(1)}, u32[]{:S(2)}, u32[]{:S(2)}) async-start(bf16[32,128,128]{2,1,0:T(8,128)(2,1)} %shard_map.178), calls=%async_computation.3 | async-start | bytes 2097152 | tf_op jit(solution)/shard_map/all_to_all | solution.py:239
  222.7 0.8 copy.29
  223.5 15.7 %all-to-all-done.3 = bf16[32,128,128]{2,1,0:T(8,128)(2,1)S(1)} async-done(((bf16[32,128,128]{2,1,0:T(8,128)(2,1)}), bf16[32,128,128]{2,1,0:T(8,128)(2,1)S(1)}, u32[]{:S(2)}, u32[]{:S(2)}) %all-to-all-start.3) | async-done | bytes 1048608 | tf_op jit(solution)/shard_map/all_to_all | solution.py:239
  239.2 0.2 pad_maximum_fusion
  239.6 3.0 %copy.25 = bf16[128,64,128]{0,2,1:T(8,128)(2,1)} copy(bf16[128,64,128]{2,0,1:T(8,128)(2,1)S(1)} %bitcast.47) | data formatting | bytes 4194304 | tf_op jit(solution)/shard_map/transpose | solution.py:240
  242.6 12.3 %fusion.8 = (f32[128,4]{0,1:T(4,128)S(1)}, f32[128,4,3072]{2,0,1:T(8,128)S(1)}) fusion(bf16[128,4,2048]{0,2,1:T(8,128)(2,1)} %bitcast.51, bf16[2048,3072]{1,0:T(8,128)(2,1)} %all-gather.2.cloned.1.call-done, f32[4,3072]{1,0:T(4,128)S(1)} %bitcast.55, bf16[1,128,4,3072]{3,2,1,0:T(4,128)(2,1)} %param.18), kind=kOutput, calls=%fused_computation.33 | convolution fusion | flops 6448741888 | bytes 24168448 | tf_op jit(solution)/shard_map/dot_general | solution.py:242
  254.8 0.8 multiply_reduce_fusion
  255.6 1.7 add_convert_fusion
  257.3 2.4 copy.27
  259.8 2.4 reshape.67
  262.2 3.0 %convolution_add_fusion = f32[512,64]{0,1:T(8,128)S(1)} fusion(bf16[512,3072]{1,0:T(8,128)(2,1)} %reshape.67, bf16[3072,64]{0,1:T(8,128)(2,1)S(1)} %copy-done, f32[64]{0:T(128)S(1)} %copy-done.11), kind=kOutput, calls=%fused_computation.6 | convolution fusion | flops 201359360 | bytes 3670272 | tf_op jit(solution)/shard_map/dot_general | solution.py:255
  265.4 2.3 collective-permute-start
  267.7 6.8 %collective-permute-done = f32[128,4,64]{2,1,0:T(4,128)S(1)} collective-permute-done((f32[128,4,64]{2,1,0:T(4,128)S(1)}, f32[128,4,64]{2,1,0:T(4,128)S(1)}, u32[]{:S(2)}, u32[]{:S(2)}) %collective-permute-start) | collective-permute-done | bytes 131104 | tf_op jit(solution)/shard_map/ppermute | solution.py:19
  274.6 0.3 multiply_subtract_fusion
  274.9 0.7 copy.31
  275.7 0.7 copy.32
  (40 shorter events, 0.7 us)
Async XLA Ops:
  7.2 255.0 %copy-start = (bf16[3072,64]{0,1:T(8,128)(2,1)S(1)}, bf16[3072,64]{0,1:T(8,128)(2,1)}, u32[]{:S(2)}) copy-start(bf16[3072,64]{0,1:T(8,128)(2,1)} %param.32) | copy-start | bytes 1179652
  7.2 235.4 %all-gather.2.cloned.1.call-start = ((), (), s32[]{:S(2)}) async-start(), calls=%async_computation.4 | async-start | bytes 12779520 | tf_op jit(solution)/shard_map/all_gather | solution.py:244
  9.4 1.6 copy-start.2
  11.0 1.6 copy-start.3
  12.6 0.9 copy-start.4
  13.5 0.9 copy-start.5
  97.7 6.0 %copy-start.10 = (s32[1,4]{1,0:T(1,128)S(1)}, s32[1,4]{1,0:T(1,128)}, u32[]{:S(2)}) copy-start(s32[1,4]{1,0:T(1,128)} %param.24) | copy-start | bytes 52
  97.7 61.9 %all-to-all-start.2 = ((bf16[32,416,128]{2,1,0:T(8,128)(2,1)}), bf16[32,416,128]{2,1,0:T(8,128)(2,1)}, u32[]{:S(2)}, u32[]{:S(2)}) async-start(bf16[32,416,128]{2,1,0:T(8,128)(2,1)} %get-tuple-element.5), calls=%async_computation.2 | async-start | bytes 6815744 | tf_op jit(solution)/shard_map/all_to_all | solution.py:235
  104.9 2.0 copy-start.1
  159.6 55.5 %all-to-all-start.1 = ((bf16[32,128,128]{2,1,0:T(8,128)(2,1)}), bf16[32,128,128]{2,1,0:T(8,128)(2,1)S(1)}, u32[]{:S(2)}, u32[]{:S(2)}) async-start(bf16[32,128,128]{2,1,0:T(8,128)(2,1)} %shard_map.177), calls=%async_computation.1 | async-start | bytes 2097152 | tf_op jit(solution)/shard_map/all_to_all | solution.py:239
  164.2 58.5 %copy-start.7 = (f32[128,4,32]{0,2,1:T(8,128)S(1)}, f32[128,4,32]{0,2,1:T(8,128)}, u32[]{:S(2)}) copy-start(f32[128,4,32]{0,2,1:T(8,128)} %param.17) | copy-start | bytes 196612
  164.2 59.3 %copy-start.9 = (f32[1,4,3072]{2,1,0:T(4,128)S(1)}, f32[1,4,3072]{2,1,0:T(4,128)}, u32[]{:S(2)}) copy-start(f32[1,4,3072]{2,1,0:T(4,128)} %param.31) | copy-start | bytes 147460
  215.0 24.2 %all-to-all-start.3 = ((bf16[32,128,128]{2,1,0:T(8,128)(2,1)}), bf16[32,128,128]{2,1,0:T(8,128)(2,1)S(1)}, u32[]{:S(2)}, u32[]{:S(2)}) async-start(bf16[32,128,128]{2,1,0:T(8,128)(2,1)} %shard_map.178), calls=%async_computation.3 | async-start | bytes 2097152 | tf_op jit(solution)/shard_map/all_to_all | solution.py:239
  239.4 3.1 %copy-start.14 = (f32[1,4,3072]{2,1,0:T(4,128)S(1)}, f32[1,4,3072]{2,1,0:T(4,128)}, u32[]{:S(2)}) copy-start(f32[1,4,3072]{2,1,0:T(4,128)} %param.29) | copy-start | bytes 147460
  254.8 0.8 copy-start.8
  259.8 2.5 copy-start.11
  262.2 5.5 %copy-start.12 = (s32[4]{0:T(128)S(1)}, s32[4]{0:T(128)}, u32[]{:S(2)}) copy-start(s32[4]{0:T(128)} %param.26) | copy-start | bytes 52
  262.2 5.5 %copy-start.13 = (s32[4]{0:T(128)S(1)}, s32[4]{0:T(128)}, u32[]{:S(2)}) copy-start(s32[4]{0:T(128)} %param.27) | copy-start | bytes 52
  262.2 12.4 %copy-start.6 = (f32[128,4,32]{2,1,0:T(4,128)S(1)}, f32[128,4,32]{2,1,0:T(4,128)}, u32[]{:S(2)}) copy-start(f32[128,4,32]{2,1,0:T(4,128)} %copy.29) | copy-start | bytes 196612
  265.4 9.2 %collective-permute-start = (f32[128,4,64]{2,1,0:T(4,128)S(1)}, f32[128,4,64]{2,1,0:T(4,128)S(1)}, u32[]{:S(2)}, u32[]{:S(2)}) collective-permute-start(f32[128,4,64]{2,1,0:T(4,128)S(1)} %bitcast.52), channel_id=1, source_target_pairs={{0,64},{64,0},{1,65},{65,1},{2,66},{66,2},{3,67},{67,3},{4,68},{68... | collective-permute-start | bytes 393224 | tf_op jit(solution)/shard_map/ppermute | solution.py:19
Sparse Core Ops, SparseCore 0:
  9.7 189.1 all-gather.1
